TPU v7x, 128 devices: a whole 4x4x4 slice. The times are simulated.
128 devices in a mesh: gx: 8 (over x_lo, z), gy: 16 (over x_hi, y, core).
Axes of the slice: x: 4 (x_hi: 2, x_lo: 2; x = x_hi * 2 + x_lo), y: 4, z: 4, core: 2. Of those that a mesh axis runs over, the one named last changes fastest.
Arguments:
- fields: float32 [14, 128, 256, 128], P(None, 'gx', 'gy'), may hold values from -0.5 to 3, as said below
- droplet_state: float32 [5, 1048576], P(None, ('gx', 'gy')), may hold values from -1 to 2, as said below
- droplet_cell: int32 [1048576], P(('gx', 'gy')), may hold values from 0 to 32767
- new_cell: int32 [1048576], P(('gx', 'gy')), may hold values from 0 to 32767
- migration_lists: int32 [512, 256], P(('gx', 'gy')), may hold values from 0 to 8191, as said below
- droplet_counts: int32 [128, 5], P(('gx', 'gy')), may hold values from 64 to 8192, as said below
Outputs:
- section_rate: float32 [14, 128, 256, 128], P(None, 'gx', 'gy')
- droplets_after: float32 [5, 1179648], P(None, ('gx', 'gy'))
- cells_after: int32 [1179648], P(('gx', 'gy'))
Inputs may be any that keep to these rules, and one draw needn't show every extreme that they name: `fields`: channel 0 (density) lies in 0.8 to 1.6, channels 1 to 3 (momentum) in -0.5 to 0.5, channel 4 (total energy) in 1.2 to 3, channels 5 to 13 (species) in 0.02 to 0.3. `droplet_state`: row 0 (mass) lies in 0.2 to 2, row 1 (temperature) in 0.5 to 1.5, rows 2 to 4 (velocity) in -1 to 1. `droplet_counts`: column 0 of row d is the number of live droplets of device d, which fill slots 0 onward; some device is full with 8192. Column 1 + r is the number leaving in direction r, from 64 to 256; every device sends exactly 256 in some direction. `migration_lists`: row 4 d + r lists, in its first droplet_counts[d, 1 + r] entries, live slots of device d leaving in direction r; no slot appears twice among a device's four rows; the remaining entries are 0.
All inputs are finite; a program needn't handle non-finite values.
Results may differ from a plain program's by a relative error of at most 0.0003.
Values sent between devices are 32-bit elements; how exact they have to be, the bound alone decides.
A program may use at most 192 MiB of HBM per device.

v0:
```python
import jax
import jax.numpy as jnp
from jax import lax
from jax.sharding import PartitionSpec as P

STENCIL = (0.8, -0.2, 4.0 / 105.0, -1.0 / 280.0)
INV_SPACING = 2.0
GAS_FACTOR = 0.4
RATE_CONST = 20.0
ACTIVATION = 2.0
REACTION_SHARES = (0.0, 0.0, 0.0, 0.0, 1.5, -1.0, -2.0, 1.5, 1.5, 0.0, 0.0, 0.0, 0.0, 0.0)
EVAP_RATE = 0.5
DRAG_RATE = 0.8
HEAT_RATE = 0.6
LATENT_HEAT = 0.3
STEP_SIZE = 0.05


def extended_2(cells, sides, width):
    for axis, dim in sides:
        count = lax.axis_size(axis)
        head = lax.slice_in_dim(cells, 0, width, axis=dim)
        tail = lax.slice_in_dim(cells, cells.shape[dim] - width, cells.shape[dim], axis=dim)
        cells = jnp.concatenate(
            [
                lax.ppermute(tail, axis, [(i, (i + 1) % count) for i in range(count)]),
                cells,
                lax.ppermute(head, axis, [((i + 1) % count, i) for i in range(count)]),
            ],
            axis=dim,
        )
    return cells


def passed_along(block, axis, distance):
    devices = range(lax.axis_size(axis))
    route = [((i - distance) % len(devices), i) for i in devices]
    return lax.ppermute(block, axis, route)


def primitives(block):
    density = block[0]
    velocity = (block[1] / density, block[2] / density, block[3] / density)
    kinetic = 0.5 * (block[1] * block[1] + block[2] * block[2] + block[3] * block[3]) / density
    temper = (block[4] - kinetic) / density
    pressure = GAS_FACTOR * density * temper
    return (density, velocity, temper, pressure)


def flux_one(block, field_index, spatial, prims):
    density, velocity, temper, pressure = prims
    along = velocity[spatial]
    flux = along * block[field_index]
    if field_index == spatial + 1:
        flux = flux + pressure
    if field_index == 4:
        flux = flux + pressure * along
    return flux


def centered(flux, dim):
    inner = flux.shape[dim] - 8
    total = jnp.zeros_like(lax.slice_in_dim(flux, 4, 4 + inner, axis=dim))
    for offset, weight in enumerate(STENCIL):
        upper = lax.slice_in_dim(flux, 5 + offset, 5 + offset + inner, axis=dim)
        lower = lax.slice_in_dim(flux, 3 - offset, 3 - offset + inner, axis=dim)
        total = total + weight * (upper - lower)
    return INV_SPACING * total


def periodic(flux, dim):
    total = jnp.zeros_like(flux)
    for offset, weight in enumerate(STENCIL):
        total = total + weight * (
            jnp.roll(flux, -(offset + 1), dim) - jnp.roll(flux, offset + 1, dim)
        )
    return INV_SPACING * total


def droplet_terms(gas, state):
    density, velocity, temper, pressure = primitives(gas)
    fuel_share = gas[5] / density
    droplet_mass = state[0]
    drop_temp = state[1]
    size = jnp.cbrt(droplet_mass)
    evap = EVAP_RATE * size * jnp.log1p(temper / (1.0 + fuel_share))
    drag = [DRAG_RATE * size * (velocity[spatial] - state[2 + spatial]) for spatial in range(3)]
    heat = HEAT_RATE * size * (temper - drop_temp)
    sources = jnp.stack(
        [
            evap,
            evap * state[2] - drag[0],
            evap * state[3] - drag[1],
            evap * state[4] - drag[2],
            evap * drop_temp - heat,
            evap,
        ]
    )
    new_state = jnp.stack(
        [
            droplet_mass - STEP_SIZE * evap,
            drop_temp + STEP_SIZE * (heat - LATENT_HEAT * evap) / droplet_mass,
            state[2] + STEP_SIZE * drag[0] / droplet_mass,
            state[3] + STEP_SIZE * drag[1] / droplet_mass,
            state[4] + STEP_SIZE * drag[2] / droplet_mass,
        ]
    )
    return (sources, new_state)


def per_device(fields, droplet_state, droplet_cell, new_cell, migration_lists, droplet_counts):
    n_fields, n_x, n_y, n_z = fields.shape
    slots = droplet_state.shape[1]
    capacity = migration_lists.shape[1]
    counts = droplet_counts[0]
    cell_count = n_x * n_y * n_z
    live = jnp.arange(slots, dtype=jnp.int32) < counts[0]
    gas = jnp.take(fields[:6].reshape(6, cell_count), droplet_cell, axis=1)
    sources, new_state = droplet_terms(gas, droplet_state)
    sources = jnp.where(live[None], sources, 0.0)
    valid = jnp.arange(capacity, dtype=jnp.int32)[None, :] < counts[1:5][:, None]
    send_state = jnp.where(valid[None], jnp.take(new_state, migration_lists, axis=1), 0.0)
    send_cell = jnp.where(valid, jnp.take(new_cell, migration_lists), -1)
    departed = (
        jnp.zeros((slots,), jnp.int32)
        .at[migration_lists.reshape(-1)]
        .add(valid.reshape(-1).astype(jnp.int32))
    )
    staying = live & (departed == 0)
    extended = extended_2(fields, (("gx", 1), ("gy", 2)), 4)
    slab_x = extended[:, :, 4 : n_y + 4]
    slab_y = extended[:, 4 : n_x + 4]
    came_state = []
    came_cell = []
    for offset, direction in ((1, 0), (-1, 1)):
        got_state, got_cell = passed_along(
            (send_state[:, direction], send_cell[direction]), "gx", offset
        )
        came_state.append(got_state)
        came_cell.append(got_cell)
    for offset, direction in ((1, 2), (-1, 3)):
        got_state, got_cell = passed_along(
            (send_state[:, direction], send_cell[direction]), "gy", offset
        )
        came_state.append(got_state)
        came_cell.append(got_cell)
    deposit = jax.vmap(
        lambda source_row: jax.ops.segment_sum(source_row, droplet_cell, num_segments=cell_count)
    )(sources)
    deposit = deposit.reshape(6, n_x, n_y, n_z)
    inner_prims = primitives(fields)
    prims_x = primitives(slab_x)
    prims_y = primitives(slab_y)
    density, velocity, temper, pressure = inner_prims
    rate = RATE_CONST * fields[5] * fields[6] / density * jnp.exp(-ACTIVATION / temper)
    rows = []
    for field_index in range(n_fields):
        along_x = centered(flux_one(slab_x, field_index, 0, prims_x), 0)
        along_y = centered(flux_one(slab_y, field_index, 1, prims_y), 1)
        along_z = periodic(flux_one(fields, field_index, 2, inner_prims), 2)
        row = -(along_x + along_y + along_z)
        if REACTION_SHARES[field_index] != 0.0:
            row = row + REACTION_SHARES[field_index] * rate
        if field_index < 6:
            row = row + deposit[field_index]
        rows.append(row)
    section_rate = jnp.stack(rows)
    own_state = jnp.where(staying[None], new_state, 0.0)
    own_cell = jnp.where(staying, new_cell, -1)
    droplets_after = jnp.concatenate([own_state] + came_state, 1)
    cells_after = jnp.concatenate([own_cell] + came_cell, 0)
    return (section_rate, droplets_after, cells_after)


def solution(mesh):
    placed = (
        P(None, "gx", "gy", None),
        P(None, ("gx", "gy")),
        P(("gx", "gy")),
        P(("gx", "gy")),
        P(("gx", "gy"), None),
        P(("gx", "gy"), None),
    )
    return jax.shard_map(
        per_device,
        mesh=mesh,
        in_specs=placed,
        out_specs=(P(None, "gx", "gy", None), P(None, ("gx", "gy")), P(("gx", "gy"))),
        check_vma=False,
    )
```

profile of v0, /device:TPU:96, one launch (start us, length us, event | category | flops | bytes accessed | tf_op | source)
XLA Modules:
  0.0 318.6 jit_solution(11452909486151116587)
XLA Ops:
  0.7 2.3 fusion.432
  3.1 1.9 collective-permute-start.1
  5.0 8.8 %copy.66 = f32[6,16,16,128]{0,3,2,1:T(8,128)} copy(f32[6,16,16,128]{3,2,1,0:T(8,128)S(1)} %slice-done) | data formatting | bytes 1572864 | tf_op jit(solution)/shard_map/slice | solution.py:118
  13.8 33.7 %gather_fusion = f32[8192,6]{1,0:T(8,128)} fusion(f32[6,32768]{0,1:T(8,128)} %bitcast.314, s32[8192]{0:T(1024)S(1)} %fusion.425), kind=kCustom, calls=%fused_computation | custom fusion | bytes 425984 | tf_op jit(solution)/shard_map/jit(_take)/gather | solution.py:118
  47.4 2.9 copy.67
  51.9 2.7 copy.69
  54.6 5.0 %gather_fusion.1 = f32[1024,5]{1,0:T(8,128)S(1)} fusion(f32[5,8192]{0,1:T(8,128)} %copy.69, s32[1024]{0:T(1024)S(1)} %broadcast_clamp_fusion), kind=kCustom, calls=%fused_computation.1 | custom fusion | bytes 45056 | tf_op jit(solution)/shard_map/jit(_take)/gather | solution.py:122
  59.8 6.2 %gather_fusion.2 = s32[1024]{0:T(1024)S(1)} fusion(s32[8192]{0:T(1024)S(1)} %copy-done, s32[1024]{0:T(1024)S(1)} %broadcast_clamp_fusion), kind=kCustom, calls=%fused_computation.2 | custom fusion | bytes 12288 | tf_op jit(solution)/shard_map/jit(_take)/gather | solution.py:123
  66.0 2.3 collective-permute-start.4
  68.4 4.1 %collective-permute-start.8 = (s32[256]{0:T(256)S(1)}, s32[256]{0:T(256)S(1)}, u32[]{:S(2)}, u32[]{:S(2)}) collective-permute-start(s32[256]{0:T(256)S(1)} %bitcast.332), channel_id=1, source_target_pairs={{112,0},{0,16},{16,32},{32,48},{48,64},{64,80},{80,96},{96,112},{1... | collective-permute-start | bytes 3080 | tf_op jit(solution)/shard_map/ppermute | solution.py:38
  106.8 0.9 fusion.478
  125.4 0.9 fusion.443
  131.3 2.7 copy.68
  134.0 51.1 %scatter_custom_fusion = f32[6,32768]{0,1:T(8,128)} fusion(s32[8192]{0:T(1024)S(1)} %copy-done.186, f32[8192,6]{1,0:T(8,128)} %copy.68, f32[]{:T(128)} %constant.29.clone.1), kind=kCustom, calls=%fused_computation.11 | custom fusion | flops 49152 | bytes 786944 | tf_op jit(solution)/shard_map/vmap()/scatter-add | solution.py:148
  185.1 57.4 %slice_reduce_fusion = (f32[32768]{0:T(1024)S(1)}, f32[32768]{0:T(1024)S(1)}, f32[32768]{0:T(1024)S(1)}, f32[32768]{0:T(1024)S(1)}, f32[32768]{0:T(1024)S(1)}, /*index=5*/f32[32768]{0:T(1024)S(1)}) fusion(f32[6,32768]{0,1:T(8,128)} %scatter_custom_fusion), kind=kLoop, calls=%fused_computation.5 | loop fusion | bytes 1572864 | tf_op jit(solution)/shard_map/slice | solution.py:165
  242.5 6.5 %scatter_custom_fusion.1 = s32[8192]{0:T(1024)S(1)} fusion(s32[1024]{0:T(1024)S(1)} %bitcast.325, s32[1024]{0:T(1024)S(1)} %bitcast.326, s32[]{:T(128)} %constant.31.clone.1), kind=kCustom, calls=%fused_computation.699 | custom fusion | flops 1024 | bytes 32772 | tf_op jit(solution)/shard_map/scatter-add | solution.py:127
  249.4 5.7 %collective-permute-done.9 = s32[256]{0:T(256)S(1)} collective-permute-done((s32[256]{0:T(256)S(1)}, s32[256]{0:T(256)S(1)}, u32[]{:S(2)}, u32[]{:S(2)}) %collective-permute-start.9) | collective-permute-done | bytes 1056 | tf_op jit(solution)/shard_map/ppermute | solution.py:38
  255.0 6.6 %collective-permute-done.10 = s32[256]{0:T(256)S(1)} collective-permute-done((s32[256]{0:T(256)S(1)}, s32[256]{0:T(256)S(1)}, u32[]{:S(2)}, u32[]{:S(2)}) %collective-permute-start.10) | collective-permute-done | bytes 1056 | tf_op jit(solution)/shard_map/ppermute | solution.py:38
  262.3 1.3 collective-permute-done.11
  263.6 5.4 %collective-permute-start.7 = (f32[5,256]{1,0:T(8,128)S(1)}, f32[5,256]{1,0:T(8,128)S(1)}, u32[]{:S(2)}, u32[]{:S(2)}) collective-permute-start(f32[5,256]{1,0:T(8,128)S(1)} %get-tuple-element.328), channel_id=1, source_target_pairs={{1,0},{2,1},{3,2},{4,3},{5,4},{6,5},{7,6},{8,7},{9,8},{10,9},{11,1... | collective-permute-start | bytes 15368 | tf_op jit(solution)/shard_map/ppermute | solution.py:38
  269.0 1.2 collective-permute-done.6
  270.4 1.2 constant_dynamic-update-slice_fusion.2
  271.8 1.1 constant_dynamic-update-slice_fusion
  273.2 5.4 %collective-permute-start.3 = (f32[14,24,4,128]{3,2,1,0:T(4,128)S(1)}, f32[14,24,4,128]{3,2,1,0:T(4,128)S(1)}, u32[]{:S(2)}, u32[]{:S(2)}) collective-permute-start(f32[14,24,4,128]{3,2,1,0:T(4,128)S(1)} %get-tuple-element.72), channel_id=1, source_target_pairs={{1,0},{2,1},{3,2},{4,3},{5,4},{6,5},{7,6},{8,7},{9,8},{10,9},{11,1... | collective-permute-start | bytes 2064392 | tf_op jit(solution)/shard_map/ppermute | solution.py:28
  278.9 8.1 %collective-permute-done.3 = f32[14,24,4,128]{3,2,1,0:T(4,128)S(1)} collective-permute-done((f32[14,24,4,128]{3,2,1,0:T(4,128)S(1)}, f32[14,24,4,128]{3,2,1,0:T(4,128)S(1)}, u32[]{:S(2)}, u32[]{:S(2)}) %collective-permute-start.3) | collective-permute-done | bytes 688160 | tf_op jit(solution)/shard_map/ppermute | solution.py:28
  287.0 5.5 %collective-permute-done.2 = f32[14,24,4,128]{3,2,1,0:T(4,128)S(1)} collective-permute-done((f32[14,24,4,128]{3,2,1,0:T(4,128)S(1)}, f32[14,24,4,128]{3,2,1,0:T(4,128)S(1)}, u32[]{:S(2)}, u32[]{:S(2)}) %collective-permute-start.2) | collective-permute-done | bytes 688160 | tf_op jit(solution)/shard_map/ppermute | solution.py:26
  295.8 1.9 fusion.282
  302.5 1.9 fusion.197
  306.6 1.8 fusion.154
  310.0 1.9 fusion.112
  313.4 1.9 fusion.72
  317.4 1.2 copy-done.189
  (520 shorter events, 74.3 us)
Async XLA Ops:
  0.6 4.4 %slice-start = ((f32[14,16,16,128]{3,2,1,0:T(8,128)}), f32[6,16,16,128]{3,2,1,0:T(8,128)S(1)}, s32[]{:S(2)}) async-start(f32[14,16,16,128]{3,2,1,0:T(8,128)} %param.6), calls=%async_computation | async-start | bytes 1572864 | tf_op jit(solution)/shard_map/slice | solution.py:118
  0.6 4.3 %copy-start.186 = (s32[8192]{0:T(1024)S(1)}, s32[8192]{0:T(1024)}, u32[]{:S(2)}) copy-start(s32[8192]{0:T(1024)} %param.8) | copy-start | bytes 98308
  2.9 267.4 %collective-permute-start = (f32[14,4,16,128]{3,2,1,0:T(8,128)}, f32[14,4,16,128]{3,2,1,0:T(8,128)}, u32[]{:S(2)}, u32[]{:S(2)}) collective-permute-start(f32[14,4,16,128]{3,2,1,0:T(8,128)} %get-tuple-element.87), channel_id=1, source_target_pairs={{0,16},{16,32},{32,48},{48,64},{64,80},{80,96},{96,112},{112,0},{1... | collective-permute-start | bytes 1376264 | tf_op jit(solution)/shard_map/ppermute | solution.py:26
  3.1 268.7 %collective-permute-start.1 = (f32[14,4,16,128]{3,2,1,0:T(8,128)}, f32[14,4,16,128]{3,2,1,0:T(8,128)}, u32[]{:S(2)}, u32[]{:S(2)}) collective-permute-start(f32[14,4,16,128]{3,2,1,0:T(8,128)} %get-tuple-element.86), channel_id=1, source_target_pairs={{16,0},{32,16},{48,32},{64,48},{80,64},{96,80},{112,96},{0,112},{1... | collective-permute-start | bytes 1376264 | tf_op jit(solution)/shard_map/ppermute | solution.py:28
  47.4 2.9 copy-start.190
  47.4 3.1 copy-start.184
  51.8 2.7 copy-start.187
  51.8 7.9 %copy-start = (s32[8192]{0:T(1024)S(1)}, s32[8192]{0:T(1024)}, u32[]{:S(2)}) copy-start(s32[8192]{0:T(1024)} %param.9) | copy-start | bytes 98308
  59.8 12.7 %copy-start.1 = (f32[14,16,16,128]{3,2,1,0:T(8,128)S(1)}, f32[14,16,16,128]{3,2,1,0:T(8,128)}, u32[]{:S(2)}) copy-start(f32[14,16,16,128]{3,2,1,0:T(8,128)} %param.6) | copy-start | bytes 5505028
  66.0 197.5 %collective-permute-start.4 = (f32[5,256]{1,0:T(8,128)S(1)}, f32[5,256]{1,0:T(8,128)S(1)}, u32[]{:S(2)}, u32[]{:S(2)}) collective-permute-start(f32[5,256]{1,0:T(8,128)S(1)} %get-tuple-element.331), channel_id=1, source_target_pairs={{112,0},{0,16},{16,32},{32,48},{48,64},{64,80},{80,96},{96,112},{1... | collective-permute-start | bytes 15368 | tf_op jit(solution)/shard_map/ppermute | solution.py:38
  68.3 200.7 %collective-permute-start.5 = (f32[5,256]{1,0:T(8,128)S(1)}, f32[5,256]{1,0:T(8,128)S(1)}, u32[]{:S(2)}, u32[]{:S(2)}) collective-permute-start(f32[5,256]{1,0:T(8,128)S(1)} %get-tuple-element.330), channel_id=1, source_target_pairs={{16,0},{32,16},{48,32},{64,48},{80,64},{96,80},{112,96},{0,112},{1... | collective-permute-start | bytes 15368 | tf_op jit(solution)/shard_map/ppermute | solution.py:38
  68.4 180.9 %collective-permute-start.8 = (s32[256]{0:T(256)S(1)}, s32[256]{0:T(256)S(1)}, u32[]{:S(2)}, u32[]{:S(2)}) collective-permute-start(s32[256]{0:T(256)S(1)} %bitcast.332), channel_id=1, source_target_pairs={{112,0},{0,16},{16,32},{32,48},{48,64},{64,80},{80,96},{96,112},{1... | collective-permute-start | bytes 3080 | tf_op jit(solution)/shard_map/ppermute | solution.py:38
  249.3 5.7 %collective-permute-start.9 = (s32[256]{0:T(256)S(1)}, s32[256]{0:T(256)S(1)}, u32[]{:S(2)}, u32[]{:S(2)}) collective-permute-start(s32[256]{0:T(256)S(1)} %bitcast.331), channel_id=1, source_target_pairs={{16,0},{32,16},{48,32},{64,48},{80,64},{96,80},{112,96},{0,112},{1... | collective-permute-start | bytes 3080 | tf_op jit(solution)/shard_map/ppermute | solution.py:38
  255.0 6.6 %collective-permute-start.10 = (s32[256]{0:T(256)S(1)}, s32[256]{0:T(256)S(1)}, u32[]{:S(2)}, u32[]{:S(2)}) collective-permute-start(s32[256]{0:T(256)S(1)} %bitcast.330), channel_id=1, source_target_pairs={{15,0},{0,1},{1,2},{2,3},{3,4},{4,5},{5,6},{6,7},{7,8},{8,9},{9,10... | collective-permute-start | bytes 3080 | tf_op jit(solution)/shard_map/ppermute | solution.py:38
  261.6 1.9 collective-permute-start.11
  263.6 6.7 %collective-permute-start.6 = (f32[5,256]{1,0:T(8,128)S(1)}, f32[5,256]{1,0:T(8,128)S(1)}, u32[]{:S(2)}, u32[]{:S(2)}) collective-permute-start(f32[5,256]{1,0:T(8,128)S(1)} %get-tuple-element.329), channel_id=1, source_target_pairs={{15,0},{0,1},{1,2},{2,3},{3,4},{4,5},{5,6},{6,7},{7,8},{8,9},{9,10... | collective-permute-start | bytes 15368 | tf_op jit(solution)/shard_map/ppermute | solution.py:38
  263.6 8.2 %copy-start.188 = (s32[9216]{0:T(1024)}, s32[9216]{0:T(1024)S(1)}, u32[]{:S(2)}) copy-start(s32[9216]{0:T(1024)S(1)} %constant_dynamic-update-slice_fusion.8) | copy-start | bytes 110596
  263.6 6.8 %collective-permute-start.7 = (f32[5,256]{1,0:T(8,128)S(1)}, f32[5,256]{1,0:T(8,128)S(1)}, u32[]{:S(2)}, u32[]{:S(2)}) collective-permute-start(f32[5,256]{1,0:T(8,128)S(1)} %get-tuple-element.328), channel_id=1, source_target_pairs={{1,0},{2,1},{3,2},{4,3},{5,4},{6,5},{7,6},{8,7},{9,8},{10,9},{11,1... | collective-permute-start | bytes 15368 | tf_op jit(solution)/shard_map/ppermute | solution.py:38
  273.2 13.8 %collective-permute-start.3 = (f32[14,24,4,128]{3,2,1,0:T(4,128)S(1)}, f32[14,24,4,128]{3,2,1,0:T(4,128)S(1)}, u32[]{:S(2)}, u32[]{:S(2)}) collective-permute-start(f32[14,24,4,128]{3,2,1,0:T(4,128)S(1)} %get-tuple-element.72), channel_id=1, source_target_pairs={{1,0},{2,1},{3,2},{4,3},{5,4},{6,5},{7,6},{8,7},{9,8},{10,9},{11,1... | collective-permute-start | bytes 2064392 | tf_op jit(solution)/shard_map/ppermute | solution.py:28
  278.6 14.0 %collective-permute-start.2 = (f32[14,24,4,128]{3,2,1,0:T(4,128)S(1)}, f32[14,24,4,128]{3,2,1,0:T(4,128)S(1)}, u32[]{:S(2)}, u32[]{:S(2)}) collective-permute-start(f32[14,24,4,128]{3,2,1,0:T(4,128)S(1)} %get-tuple-element.71), channel_id=1, source_target_pairs={{0,1},{1,2},{2,3},{3,4},{4,5},{5,6},{6,7},{7,8},{8,9},{9,10},{10,1... | collective-permute-start | bytes 2064392 | tf_op jit(solution)/shard_map/ppermute | solution.py:26
  302.4 2.1 copy-start.142
  302.4 2.1 copy-start.143
  302.4 2.1 copy-start.148
  302.5 2.1 copy-start.149
  302.5 2.1 copy-start.154
  302.5 2.1 copy-start.155
  302.5 2.1 copy-start.158
  302.5 2.1 copy-start.159
  302.5 2.1 copy-start.162
  302.5 2.1 copy-start.163
  302.5 2.1 copy-start.166
  302.5 2.1 copy-start.167
  (172 other events, 257.7 us)
where the time goes:
time: 319 us
  local copies, waits for them, and re-layouts  194 us (61%)
  other arithmetic  73.5 us (23%)
  waiting for transfers between devices  28.5 us (9%)
  starting transfers between devices  20 us (6%)
    slice x72, local copies, waits for them, and re-layouts, periodic(): jnp.roll(flux, offset + 1, dim)  58.3 us
    slice x1, local copies, waits for them, and re-layouts, per_device(): row = row + deposit[field_index]  57.4 us
    scatter-add x1, other arithmetic, per_device(): jax.ops.segment_sum(source_row, droplet_cell, num_segments=cell_count)  51.1 us
    gather x2, local copies, waits for them, and re-layouts, per_device(): gas = jnp.take(fields[:6].reshape(6, cell_count), droplet_cell, axis=1)  36.5 us
    ppermute x8, waiting for transfers between devices, passed_along(): return lax.ppermute(block, axis, route)  14.9 us
    unnamed x16, other arithmetic  12.9 us
    ppermute x8, starting transfers between devices, passed_along(): return lax.ppermute(block, axis, route)  12.6 us
    unnamed x393, local copies, waits for them, and re-layouts  11.6 us
  transfers between devices with their start and end apart: 12, of which 7 were waited for; matrix products, arithmetic and copies ran while one was open for 75% of the time, Pallas kernels for 0%

commit v1 on v0

v1 whole, which is shorter than its diff:
```python
import functools

import jax
import jax.numpy as jnp
from jax import lax
from jax.experimental import pallas as pl
from jax.experimental.pallas import tpu as pltpu
from jax.sharding import PartitionSpec as P

F32 = jnp.float32
BF16 = jnp.bfloat16
I32 = jnp.int32
MESH = pl.DeviceIdType.MESH

STENCIL = (1.6, -0.4, 8.0 / 105.0, -1.0 / 140.0)
SHARES = (0.0, 0.0, 0.0, 0.0, 1.5, -1.0, -2.0, 1.5, 1.5, 0.0, 0.0, 0.0, 0.0, 0.0)
N_F = 14
SLOTS = 8192
ROWS = SLOTS // 128
CAP = 256
TILE = 512


def split(value):
    high = value.astype(BF16)
    low = (value - high.astype(F32)).astype(BF16)
    return high, low


def primitives(q):
    inverse = 1.0 / q[0]
    u = (q[1] * inverse, q[2] * inverse, q[3] * inverse)
    kinetic = 0.5 * (q[1] * q[1] + q[2] * q[2] + q[3] * q[3]) * inverse
    temper = (q[4] - kinetic) * inverse
    return inverse, u, temper, 0.4 * q[0] * temper


def evap_log(temper, q5, inverse):
    return 0.5 * jnp.log(1.0 + temper / (1.0 + q5 * inverse))


def flux(f, axis, value, u, p):
    result = u * value
    if f == axis + 1:
        result = result + p
    if f == 4:
        result = result + p * u
    return result


def gather_kernel(
    n_gx, n_gy,
    fields, fields_y, state, cell_h, new_cell_h, lists_h, counts_h,
    fv, xh, yh, arr, own, own_cell, dep,
    cell, new_cell, lists, counts, st, table, s5, sv, gas, ns, msg,
    in_sem, send_sem, recv_sem,
):
    gx = lax.axis_index("gx")
    gy = lax.axis_index("gy")
    x_next = (lax.rem(gx + 1, n_gx), gy)
    x_prev = (lax.rem(gx + n_gx - 1, n_gx), gy)
    y_next = (gx, lax.rem(gy + 1, n_gy))
    y_prev = (gx, lax.rem(gy + n_gy - 1, n_gy))
    targets = (x_next, x_prev, y_next, y_prev)
    barrier = pltpu.get_barrier_semaphore()
    for device in targets:
        pl.semaphore_signal(barrier, inc=1, device_id=device, device_id_type=MESH)
    loads = [
        pltpu.make_async_copy(src, dst, in_sem.at[i])
        for i, (src, dst) in enumerate(
            (
                (state, st),
                (cell_h, cell),
                (new_cell_h, new_cell),
                (lists_h, lists),
                (counts_h, counts),
                (fields, fv),
            )
        )
    ]
    for copy in loads:
        copy.start()
    pl.semaphore_wait(barrier, 4)
    n_x = fields.shape[1]
    faces = (
        (fields.at[:, n_x - 4 : n_x], xh.at[0]),
        (fields.at[:, 0:4], xh.at[1]),
        (fields_y.at[:, :, 3], yh.at[:, :, 1]),
        (fields_y.at[:, :, 0], yh.at[:, :, 0]),
    )
    sends = [
        pltpu.make_async_remote_copy(
            src_ref=src,
            dst_ref=dst,
            send_sem=send_sem.at[i],
            recv_sem=recv_sem.at[i],
            device_id=targets[i],
            device_id_type=MESH,
        )
        for i, (src, dst) in enumerate(faces)
    ]
    for copy in sends:
        copy.start()
    for copy in loads:
        copy.wait()

    for i in range(ROWS):
        for k in range(5):
            s5[k, i : i + 1, :] = st[k : k + 1, i * 128 : (i + 1) * 128]
    slot = lax.broadcasted_iota(I32, (ROWS, 128), 0) * 128 + lax.broadcasted_iota(
        I32, (ROWS, 128), 1
    )
    live = slot < counts[0:1, 0:1]
    mass = s5[0]
    theta = s5[1]
    size = jnp.exp(jnp.log(mass) * (1.0 / 3.0))
    live_size = jnp.where(live, size, 0.0)
    weights = (
        live_size,
        live_size * s5[2],
        live_size * s5[3],
        live_size * s5[4],
        live_size * theta,
    )
    for k, value in enumerate(weights):
        high, low = split(value)
        sv[k] = high.astype(F32)
        sv[5 + k] = low.astype(F32)

    for h in range(2):
        q = [fv[f, 8 * h : 8 * h + 8].reshape(128, 128) for f in range(6)]
        inverse, u, temper, _ = primitives(q)
        values = (u[0], u[1], u[2], temper, evap_log(temper, q[5], inverse))
        for k, value in enumerate(values):
            high, low = split(value)
            table[k * 128 : (k + 1) * 128, h * 128 : h * 128 + 128] = high
            table[k * 128 : (k + 1) * 128, 256 + h * 128 : 384 + h * 128] = low

    per = TILE // 128
    column_ids = lax.broadcasted_iota(I32, (256, 128), 0)
    row_ids = lax.broadcasted_iota(I32, (128, 128), 0)

    def one_hots(t):
        hots = []
        masks = []
        for j in range(per):
            c = cell[pl.ds(t * per + j, 1), :]
            column = lax.shift_left(lax.shift_right_logical(c, 14), 7) + (c & 127)
            row = lax.shift_right_logical(c, 7) & 127
            hots.append(jnp.where(column_ids == column, 1.0, 0.0).astype(BF16))
            masks.append(row_ids == row)
        return hots, masks

    def gather_step(t, carry):
        hots, masks = one_hots(t)
        for j in range(0, per, 2):
            hot = jnp.concatenate(hots[j : j + 2], 1)
            hot = jnp.concatenate([hot, hot], 0)
            mask = jnp.concatenate(masks[j : j + 2], 1)
            for k in range(5):
                rows = jnp.dot(
                    table[k * 128 : (k + 1) * 128, :], hot, preferred_element_type=F32
                )
                got = jnp.sum(jnp.where(mask, rows, 0.0), axis=0, keepdims=True)
                gas[k, pl.ds(t * per + j, 1), :] = got[:, :128]
                gas[k, pl.ds(t * per + j + 1, 1), :] = got[:, 128:]
        return carry

    lax.fori_loop(0, ROWS // per, gather_step, 0)

    inv_mass = 1.0 / mass
    evap = size * gas[4]
    heat = 0.6 * size * (gas[3] - theta)
    new_state = [
        mass - 0.05 * evap,
        theta + 0.05 * (heat - 0.3 * evap) * inv_mass,
    ]
    for a in range(3):
        v = s5[2 + a]
        new_state.append(v + 0.04 * size * (gas[a] - v) * inv_mass)
    for k in range(5):
        high, low = split(new_state[k])
        ns[k * ROWS : (k + 1) * ROWS, 0:128] = high
        ns[k * ROWS : (k + 1) * ROWS, 128:256] = low
    cells = new_cell[...]
    cell_high = lax.shift_left(lax.shift_right_logical(cells, 8), 8)
    ns[5 * ROWS : 6 * ROWS, 0:128] = cell_high.astype(F32).astype(BF16)
    ns[5 * ROWS : 6 * ROWS, 128:256] = (cells & 255).astype(F32).astype(BF16)

    entry = lax.broadcasted_iota(I32, (1, CAP), 1)
    slot_rows = lax.broadcasted_iota(I32, (ROWS, CAP), 0)
    slot_lanes = lax.broadcasted_iota(I32, (128, CAP), 0)
    departed = jnp.zeros((ROWS, 128), F32)
    for r in range(4):
        picked = lists[r : r + 1, :]
        valid = entry < counts[0:1, 1 + r : 2 + r]
        row_mask = slot_rows == lax.shift_right_logical(picked, 7)
        lane_hot = jnp.where(slot_lanes == (picked & 127), 1.0, 0.0).astype(BF16)
        row_hot = jnp.where(row_mask & valid, 1.0, 0.0).astype(BF16)
        departed += lax.dot_general(
            row_hot, lane_hot, (((1,), (1,)), ((), ())), preferred_element_type=F32
        )
        rows = jnp.dot(
            ns[...], jnp.concatenate([lane_hot, lane_hot], 0), preferred_element_type=F32
        )
        for k in range(6):
            got = jnp.sum(
                jnp.where(row_mask, rows[k * ROWS : (k + 1) * ROWS], 0.0), axis=0, keepdims=True
            )
            msg[r, k : k + 1, :] = jnp.where(valid, got, 0.0 if k < 5 else -1.0)
        msg[r, 6:8, :] = jnp.zeros((2, CAP), F32)
        copy = pltpu.make_async_remote_copy(
            src_ref=msg.at[r],
            dst_ref=arr.at[r],
            send_sem=send_sem.at[4 + r],
            recv_sem=recv_sem.at[4 + r],
            device_id=targets[r],
            device_id_type=MESH,
        )
        copy.start()
        sends.append(copy)
    staying = live & (departed == 0.0)
    own_cell[...] = jnp.where(staying, cells, -1)
    for k in range(5):
        gas[k] = jnp.where(staying, new_state[k], 0.0)
    for i in range(ROWS):
        for k in range(5):
            own[k : k + 1, i * 128 : (i + 1) * 128] = gas[k, i : i + 1, :]

    dep[...] = jnp.zeros_like(dep)

    def deposit_step(t, carry):
        hots, masks = one_hots(t)
        hot = jnp.concatenate(hots + hots, 1)
        for k in range(5):
            parts = [
                jnp.where(masks[j], sv[part + k, pl.ds(t * per + j, 1), :], 0.0).astype(BF16)
                for part in (0, 5)
                for j in range(per)
            ]
            dep[k] += lax.dot_general(
                jnp.concatenate(parts, 1),
                hot,
                (((1,), (1,)), ((), ())),
                preferred_element_type=F32,
            )
        return carry

    lax.fori_loop(0, ROWS // per, deposit_step, 0)
    for copy in sends:
        copy.wait()


def stencil_kernel(
    fv, xh, yh, dep, own, own_cell, arr,
    out, drops, cells,
    uv, pv, wv, ux, px, uy, py, fx, fy,
):
    drops[:, 0:SLOTS] = own[...]
    cells[0:ROWS, :] = own_cell[...]
    for r in range(4):
        drops[:, SLOTS + CAP * r : SLOTS + CAP * (r + 1)] = arr[r, 0:5, :]
        for j in range(2):
            row = ROWS + 2 * r + j
            cells[row : row + 1, :] = arr[r, 5:6, 128 * j : 128 * j + 128].astype(I32)

    def cell_step(x, carry):
        q = [fv[f, x] for f in range(7)]
        inverse, u, temper, p = primitives(q)
        for a in range(3):
            uv[a, x] = u[a]
        pv[x] = p
        wv[x] = 20.0 * q[5] * q[6] * inverse * jnp.exp(-2.0 / temper)
        log = evap_log(temper, q[5], inverse)
        rows = pl.ds(pl.multiple_of(lax.rem(x, 8) * 16, 16), 16)
        lanes = pl.ds(pl.multiple_of(lax.div(x, 8) * 128, 128), 128)
        sums = [dep[k, rows, lanes] for k in range(5)]
        evap = log * sums[0]
        out[0, x] = evap
        out[5, x] = evap
        for a in range(3):
            out[1 + a, x] = (log + 0.8) * sums[1 + a] - 0.8 * u[a] * sums[0]
        out[4, x] = (log + 0.6) * sums[4] - 0.6 * temper * sums[0]
        _, u, _, p = primitives([yh[f, x] for f in range(5)])
        uy[x] = u[1]
        py[x] = p
        return carry

    lax.fori_loop(0, 16, cell_step, 0, unroll=2)
    for s in range(2):
        for i in range(4):
            _, u, _, p = primitives([xh[s, f, i] for f in range(5)])
            ux[s, i] = u[0]
            px[s, i] = p

    for f in range(N_F):
        for s in range(2):
            for i in range(4):
                fx[20 * s + i] = flux(f, 0, xh[s, f, i], ux[s, i], px[s, i])

        def flux_step(x, carry):
            value = fv[f, x]
            fx[4 + x] = flux(f, 0, value, uv[0, x], pv[x])
            edge = flux(f, 1, yh[f, x], uy[x], py[x])
            fy[x, 8:24] = flux(f, 1, value, uv[1, x], pv[x])
            fy[x, 4:8] = edge[4:8]
            fy[x, 24:28] = edge[0:4]
            return carry

        lax.fori_loop(0, 16, flux_step, 0, unroll=8)

        def rate_step(x, carry):
            fz = flux(f, 2, fv[f, x], uv[2, x], pv[x])
            total = None
            for k in range(4):
                term = (
                    (fx[x + 5 + k] - fx[x + 3 - k])
                    + (fy[x, 9 + k : 25 + k] - fy[x, 7 - k : 23 - k])
                    + (pltpu.roll(fz, 127 - k, 1) - pltpu.roll(fz, k + 1, 1))
                )
                total = STENCIL[k] * term if total is None else total + STENCIL[k] * term
            row = -total
            if SHARES[f] != 0.0:
                row = row + SHARES[f] * wv[x]
            if f < 6:
                row = row + out[f, x]
            out[f, x] = row
            return carry

        lax.fori_loop(0, 16, rate_step, 0, unroll=8)


def shape(dims, dtype=F32):
    return jax.ShapeDtypeStruct(dims, dtype)


def per_device(n_gx, n_gy, fields, state, cell, new_cell, lists, counts):
    n_f, n_x, n_y, n_z = fields.shape
    vmem = pl.BlockSpec(memory_space=pltpu.VMEM)
    hbm = pl.BlockSpec(memory_space=pltpu.HBM)
    fv, xh, yh, arr, own, own_cell, dep = pl.pallas_call(
        functools.partial(gather_kernel, n_gx, n_gy),
        out_shape=(
            shape((n_f, n_x, n_y, n_z)),
            shape((2, n_f, 4, n_y, n_z)),
            shape((n_f, n_x, 2, 4, n_z)),
            shape((4, 8, CAP)),
            shape((5, SLOTS)),
            shape((ROWS, 128), I32),
            shape((5, 128, 256)),
        ),
        in_specs=[hbm] * 7,
        out_specs=(vmem,) * 7,
        scratch_shapes=[
            pltpu.VMEM((ROWS, 128), I32),
            pltpu.VMEM((ROWS, 128), I32),
            pltpu.VMEM((4, CAP), I32),
            pltpu.VMEM((1, 5), I32),
            pltpu.VMEM((5, SLOTS), F32),
            pltpu.VMEM((640, 512), BF16),
            pltpu.VMEM((5, ROWS, 128), F32),
            pltpu.VMEM((10, ROWS, 128), F32),
            pltpu.VMEM((5, ROWS, 128), F32),
            pltpu.VMEM((6 * ROWS, 256), BF16),
            pltpu.VMEM((4, 8, CAP), F32),
            pltpu.SemaphoreType.DMA((6,)),
            pltpu.SemaphoreType.DMA((8,)),
            pltpu.SemaphoreType.DMA((8,)),
        ],
        compiler_params=pltpu.CompilerParams(
            collective_id=0, has_side_effects=True, vmem_limit_bytes=24 << 20
        ),
        name="droplets",
    )(
        *(
            pltpu.with_memory_space_constraint(a, pltpu.HBM)
            for a in (
                fields,
                fields.reshape(n_f, n_x, n_y // 4, 4, n_z),
                state,
                cell.reshape(ROWS, 128),
                new_cell.reshape(ROWS, 128),
                lists,
                counts,
            )
        )
    )
    out, drops, cells = pl.pallas_call(
        stencil_kernel,
        grid=(1,),
        out_shape=(
            shape((n_f, n_x, n_y, n_z)),
            shape((5, SLOTS + 4 * CAP)),
            shape((ROWS + 8, 128), I32),
        ),
        in_specs=[vmem] * 7,
        out_specs=tuple(
            pl.BlockSpec(s, lambda i, n=len(s): (0,) * n)
            for s in ((n_f, n_x, n_y, n_z), (5, SLOTS + 4 * CAP), (ROWS + 8, 128))
        ),
        scratch_shapes=[
            pltpu.VMEM((3, 16, 16, 128), F32),
            pltpu.VMEM((16, 16, 128), F32),
            pltpu.VMEM((16, 16, 128), F32),
            pltpu.VMEM((2, 4, 16, 128), F32),
            pltpu.VMEM((2, 4, 16, 128), F32),
            pltpu.VMEM((16, 8, 128), F32),
            pltpu.VMEM((16, 8, 128), F32),
            pltpu.VMEM((24, 16, 128), F32),
            pltpu.VMEM((16, 32, 128), F32),
        ],
        compiler_params=pltpu.CompilerParams(vmem_limit_bytes=24 << 20),
        name="stencil",
    )(fv, xh, yh.reshape(n_f, n_x, 8, n_z), dep, own, own_cell, arr)
    return out, drops, cells.reshape(-1)


def solution(mesh):
    placed = (
        P(None, "gx", "gy", None),
        P(None, ("gx", "gy")),
        P(("gx", "gy")),
        P(("gx", "gy")),
        P(("gx", "gy"), None),
        P(("gx", "gy"), None),
    )
    return jax.shard_map(
        functools.partial(per_device, mesh.shape["gx"], mesh.shape["gy"]),
        mesh=mesh,
        in_specs=placed,
        out_specs=(P(None, "gx", "gy", None), P(None, ("gx", "gy")), P(("gx", "gy"))),
        check_vma=False,
    )
```

time: 319 us -> 40.3 us (0.13)
  local copies, waits for them, and re-layouts: 194 us -> 0 us
  other arithmetic: 73.5 us -> 0 us
  Pallas kernels: 0 us -> 39 us
  waiting for transfers between devices: 28.5 us -> 0 us
  starting transfers between devices: 20 us -> 0 us
    slice x79 -> x0, local copies, waits for them, and re-layouts: 127 us -> none  [the longest x72 58.3 us: periodic(): jnp.roll(flux, offset + 1, dim)]
    scatter-add x2 -> x0, other arithmetic: 57.6 us -> none  [the longest x1 51.1 us: per_device(): jax.ops.segment_sum(source_row, droplet_cell, num_segments=cell_count)]
    gather x6 -> x0, local copies, waits for them, and re-layouts: 47.9 us -> none  [the longest x2 36.5 us: per_device(): gas = jnp.take(fields[:6].reshape(6, cell_count), droplet_cell, axis=1)]
    pallas_call x0 -> x2, Pallas kernels: none -> 39 us  [the longest x1 31 us: per_device(): pl.pallas_call(functools.partial(gather_kernel, n_gx, n_gy), out_shape=(s...]
    ppermute x12 -> x0, waiting for transfers between devices: 28.5 us -> none  [the longest x8 14.9 us: passed_along(): return lax.ppermute(block, axis, route)]
    ppermute x12 -> x0, starting transfers between devices: 20 us -> none  [the longest x8 12.6 us: passed_along(): return lax.ppermute(block, axis, route)]
    unnamed x16 -> x0, other arithmetic: 12.9 us -> none
    unnamed x393 -> x0, local copies, waits for them, and re-layouts: 11.6 us -> none
  transfers between devices with their start and end apart: 12 -> 0, of which waited for: 7 -> 0; matrix products, arithmetic and copies ran while one was open for 75% -> 0% of each run, Pallas kernels for 0% -> 0%
where the time goes in v1:
time: 40.3 us; the launch traced here: 39.6 us
  Pallas kernels  39 us (97%)
  between operations  0.64 us (2%)
    pallas_call x1, Pallas kernels, per_device(): pl.pallas_call(functools.partial(gather_kernel, n_gx, n_gy), out_shape=(s...  31 us
    pallas_call x1, Pallas kernels, per_device(): pl.pallas_call(stencil_kernel, grid=(1,), out_shape=(shape((n_f, n_x, n_y...  7.96 us

profile of v1, /device:TPU:96, one launch (start us, length us, event | category | flops | bytes accessed | tf_op | source)
XLA Modules:
  0.0 39.6 jit_solution(10166003986075587280)
XLA Ops:
  0.6 31.0 %droplets.1 = (f32[14,16,16,128]{3,2,1,0:T(8,128)S(1)}, f32[2,14,4,16,128]{4,3,2,1,0:T(8,128)S(1)}, f32[14,16,2,4,128]{4,3,2,1,0:T(4,128)S(1)}, f32[4,8,256]{2,1...) custom-call(f32[14,16,16,128]{3,2,1,0:T(8,128)} %fields.1, ...), custom_call_target="tpu_custom_call" | custom-call | tf_op jit(solution)/shard_map/droplets/pallas_call | solution.py:341
  31.7 8.0 %stencil.1 = (f32[14,16,16,128]{3,2,1,0:T(8,128)}, f32[5,9216]{1,0:T(8,128)}, s32[72,128]{1,0:T(8,128)}) custom-call(f32[14,16,16,128]{3,2,1,0:T(8,128)S(1)} %get-tuple-element.13.fv, f32[2,14,4,16,128]{4,3,2,1,0:T(8,128)S(1)} %get-tuple-element.14.xh, f32[14,16,8,128]{3,2,1,0:T(8,128)S(1)} %bitcast.5, f32[5,128,256]{2,1,0:T(8,128)S(1)} %get-tuple-element.16.dep, ...), custom_call_target="tpu_custom_call" | custom-call | tf_op jit(solution)/shard_map/stencil/pallas_call | solution.py:388

commit v2 on v1

--- a/solution.py
+++ b/solution.py
@@ -18,7 +18,7 @@
 SLOTS = 8192
 ROWS = SLOTS // 128
 CAP = 256
-TILE = 512
+TILE = 1024
 
 
 def split(value):
@@ -48,11 +48,12 @@
     return result
 
 
-def gather_kernel(
+def droplet_kernel(
     n_gx, n_gy,
     fields, fields_y, state, cell_h, new_cell_h, lists_h, counts_h,
-    fv, xh, yh, arr, own, own_cell, dep,
-    cell, new_cell, lists, counts, st, table, s5, sv, gas, ns, msg,
+    part, xh, yh, arr, own, own_cell,
+    fv, cell, new_cell, lists, counts, st, table, s5, sv, gas, ns, msg, dep,
+    uv, pv, wv, fx, fy,
     in_sem, send_sem, recv_sem,
 ):
     gx = lax.axis_index("gx")
@@ -139,8 +140,9 @@
     per = TILE // 128
     column_ids = lax.broadcasted_iota(I32, (256, 128), 0)
     row_ids = lax.broadcasted_iota(I32, (128, 128), 0)
-
-    def one_hots(t):
+    dep[...] = jnp.zeros_like(dep)
+
+    def droplet_step(t, carry):
         hots = []
         masks = []
         for j in range(per):
@@ -149,24 +151,37 @@
             row = lax.shift_right_logical(c, 7) & 127
             hots.append(jnp.where(column_ids == column, 1.0, 0.0).astype(BF16))
             masks.append(row_ids == row)
-        return hots, masks
-
-    def gather_step(t, carry):
-        hots, masks = one_hots(t)
         for j in range(0, per, 2):
             hot = jnp.concatenate(hots[j : j + 2], 1)
-            hot = jnp.concatenate([hot, hot], 0)
+            rows = jnp.dot(
+                table[...], jnp.concatenate([hot, hot], 0), preferred_element_type=F32
+            )
             mask = jnp.concatenate(masks[j : j + 2], 1)
             for k in range(5):
-                rows = jnp.dot(
-                    table[k * 128 : (k + 1) * 128, :], hot, preferred_element_type=F32
+                got = jnp.sum(
+                    jnp.where(mask, rows[k * 128 : (k + 1) * 128], 0.0), axis=0, keepdims=True
                 )
-                got = jnp.sum(jnp.where(mask, rows, 0.0), axis=0, keepdims=True)
                 gas[k, pl.ds(t * per + j, 1), :] = got[:, :128]
                 gas[k, pl.ds(t * per + j + 1, 1), :] = got[:, 128:]
+        lefts = []
+        for k in range(5):
+            parts = [
+                jnp.where(masks[j], sv[half + k, pl.ds(t * per + j, 1), :], 0.0).astype(BF16)
+                for half in (0, 5)
+                for j in range(per)
+            ]
+            lefts.append(jnp.concatenate(parts, 1))
+        sums = lax.dot_general(
+            jnp.concatenate(lefts, 0),
+            jnp.concatenate(hots + hots, 1),
+            (((1,), (1,)), ((), ())),
+            preferred_element_type=F32,
+        )
+        for k in range(5):
+            dep[k] += sums[k * 128 : (k + 1) * 128]
         return carry
 
-    lax.fori_loop(0, ROWS // per, gather_step, 0)
+    lax.fori_loop(0, ROWS // per, droplet_step, 0)
 
     inv_mass = 1.0 / mass
     evap = size * gas[4]
@@ -227,43 +242,6 @@
         for k in range(5):
             own[k : k + 1, i * 128 : (i + 1) * 128] = gas[k, i : i + 1, :]
 
-    dep[...] = jnp.zeros_like(dep)
-
-    def deposit_step(t, carry):
-        hots, masks = one_hots(t)
-        hot = jnp.concatenate(hots + hots, 1)
-        for k in range(5):
-            parts = [
-                jnp.where(masks[j], sv[part + k, pl.ds(t * per + j, 1), :], 0.0).astype(BF16)
-                for part in (0, 5)
-                for j in range(per)
-            ]
-            dep[k] += lax.dot_general(
-                jnp.concatenate(parts, 1),
-                hot,
-                (((1,), (1,)), ((), ())),
-                preferred_element_type=F32,
-            )
-        return carry
-
-    lax.fori_loop(0, ROWS // per, deposit_step, 0)
-    for copy in sends:
-        copy.wait()
-
-
-def stencil_kernel(
-    fv, xh, yh, dep, own, own_cell, arr,
-    out, drops, cells,
-    uv, pv, wv, ux, px, uy, py, fx, fy,
-):
-    drops[:, 0:SLOTS] = own[...]
-    cells[0:ROWS, :] = own_cell[...]
-    for r in range(4):
-        drops[:, SLOTS + CAP * r : SLOTS + CAP * (r + 1)] = arr[r, 0:5, :]
-        for j in range(2):
-            row = ROWS + 2 * r + j
-            cells[row : row + 1, :] = arr[r, 5:6, 128 * j : 128 * j + 128].astype(I32)
-
     def cell_step(x, carry):
         q = [fv[f, x] for f in range(7)]
         inverse, u, temper, p = primitives(q)
@@ -276,35 +254,26 @@
         lanes = pl.ds(pl.multiple_of(lax.div(x, 8) * 128, 128), 128)
         sums = [dep[k, rows, lanes] for k in range(5)]
         evap = log * sums[0]
-        out[0, x] = evap
-        out[5, x] = evap
+        part[0, x] = evap
+        part[5, x] = evap
         for a in range(3):
-            out[1 + a, x] = (log + 0.8) * sums[1 + a] - 0.8 * u[a] * sums[0]
-        out[4, x] = (log + 0.6) * sums[4] - 0.6 * temper * sums[0]
-        _, u, _, p = primitives([yh[f, x] for f in range(5)])
-        uy[x] = u[1]
-        py[x] = p
+            part[1 + a, x] = (log + 0.8) * sums[1 + a] - 0.8 * u[a] * sums[0]
+        part[4, x] = (log + 0.6) * sums[4] - 0.6 * temper * sums[0]
         return carry
 
     lax.fori_loop(0, 16, cell_step, 0, unroll=2)
-    for s in range(2):
-        for i in range(4):
-            _, u, _, p = primitives([xh[s, f, i] for f in range(5)])
-            ux[s, i] = u[0]
-            px[s, i] = p
-
+    blank = jnp.zeros((4, 16, 128), F32)
+    fx[0:4] = blank
+    fx[20:24] = blank
+    for x in range(16):
+        fy[x, 0:8] = jnp.zeros((8, 128), F32)
+        fy[x, 24:32] = jnp.zeros((8, 128), F32)
     for f in range(N_F):
-        for s in range(2):
-            for i in range(4):
-                fx[20 * s + i] = flux(f, 0, xh[s, f, i], ux[s, i], px[s, i])
 
         def flux_step(x, carry):
             value = fv[f, x]
             fx[4 + x] = flux(f, 0, value, uv[0, x], pv[x])
-            edge = flux(f, 1, yh[f, x], uy[x], py[x])
             fy[x, 8:24] = flux(f, 1, value, uv[1, x], pv[x])
-            fy[x, 4:8] = edge[4:8]
-            fy[x, 24:28] = edge[0:4]
             return carry
 
         lax.fori_loop(0, 16, flux_step, 0, unroll=8)
@@ -323,11 +292,82 @@
             if SHARES[f] != 0.0:
                 row = row + SHARES[f] * wv[x]
             if f < 6:
-                row = row + out[f, x]
-            out[f, x] = row
+                row = row + part[f, x]
+            part[f, x] = row
             return carry
 
         lax.fori_loop(0, 16, rate_step, 0, unroll=8)
+    for copy in sends:
+        copy.wait()
+
+
+def edge_kernel(
+    part, xh, yh, own, own_cell, arr,
+    out_h, drops_h, cells_h,
+    out, drops, cells, ux, px, uy, py, sem,
+):
+    drops[:, 0:SLOTS] = own[...]
+    cells[0:ROWS, :] = own_cell[...]
+    for r in range(4):
+        drops[:, SLOTS + CAP * r : SLOTS + CAP * (r + 1)] = arr[r, 0:5, :]
+        for j in range(2):
+            row = ROWS + 2 * r + j
+            cells[row : row + 1, :] = arr[r, 5:6, 128 * j : 128 * j + 128].astype(I32)
+    copies = [
+        pltpu.make_async_copy(drops, drops_h, sem.at[N_F]),
+        pltpu.make_async_copy(cells, cells_h, sem.at[N_F + 1]),
+    ]
+    for copy in copies:
+        copy.start()
+
+    def cell_step(x, carry):
+        _, u, _, p = primitives([yh[f, x] for f in range(5)])
+        uy[x] = u[1]
+        py[x] = p
+        return carry
+
+    lax.fori_loop(0, 16, cell_step, 0, unroll=4)
+    for s in range(2):
+        for i in range(4):
+            _, u, _, p = primitives([xh[s, f, i] for f in range(5)])
+            ux[s, i] = u[0]
+            px[s, i] = p
+
+    row = lax.broadcasted_iota(I32, (8, 128), 0)
+    zero = jnp.zeros((8, 128), F32)
+    down = [jnp.where(row < k + 1, -STENCIL[k], 0.0) for k in range(4)]
+    up = [jnp.where(row >= 7 - k, STENCIL[k], 0.0) for k in range(4)]
+    for f in range(N_F):
+
+        def y_step(x, carry):
+            edge = flux(f, 1, yh[f, x], uy[x], py[x])
+            total = (down[3] + up[3]) * pltpu.roll(edge, 4, 0)
+            for k in range(3):
+                total = total + down[k] * pltpu.roll(edge, k + 1, 0)
+                total = total + up[k] * pltpu.roll(edge, 7 - k, 0)
+            out[f, x, 0:8] = part[f, x, 0:8] - jnp.where(row < 4, total, zero)
+            out[f, x, 8:16] = part[f, x, 8:16] - jnp.where(row < 4, zero, total)
+            return carry
+
+        lax.fori_loop(0, 16, y_step, 0, unroll=8)
+        low = [flux(f, 0, xh[0, f, i], ux[0, i], px[0, i]) for i in range(4)]
+        high = [flux(f, 0, xh[1, f, i], ux[1, i], px[1, i]) for i in range(4)]
+        for x in range(4):
+            total = None
+            for k in range(x, 4):
+                term = STENCIL[k] * low[3 + x - k]
+                total = term if total is None else total + term
+            out[f, x] += total
+            total = None
+            for k in range(x, 4):
+                term = STENCIL[k] * high[k - x]
+                total = term if total is None else total + term
+            out[f, 15 - x] -= total
+        copy = pltpu.make_async_copy(out.at[f], out_h.at[f], sem.at[f])
+        copy.start()
+        copies.append(copy)
+    for copy in copies:
+        copy.wait()
 
 
 def shape(dims, dtype=F32):
@@ -338,20 +378,21 @@
     n_f, n_x, n_y, n_z = fields.shape
     vmem = pl.BlockSpec(memory_space=pltpu.VMEM)
     hbm = pl.BlockSpec(memory_space=pltpu.HBM)
-    fv, xh, yh, arr, own, own_cell, dep = pl.pallas_call(
-        functools.partial(gather_kernel, n_gx, n_gy),
+    cube = (n_x, n_y, n_z)
+    part, xh, yh, arr, own, own_cell = pl.pallas_call(
+        functools.partial(droplet_kernel, n_gx, n_gy),
         out_shape=(
-            shape((n_f, n_x, n_y, n_z)),
+            shape((n_f,) + cube),
             shape((2, n_f, 4, n_y, n_z)),
             shape((n_f, n_x, 2, 4, n_z)),
             shape((4, 8, CAP)),
             shape((5, SLOTS)),
             shape((ROWS, 128), I32),
-            shape((5, 128, 256)),
         ),
         in_specs=[hbm] * 7,
-        out_specs=(vmem,) * 7,
+        out_specs=(vmem,) * 6,
         scratch_shapes=[
+            pltpu.VMEM((n_f,) + cube, F32),
             pltpu.VMEM((ROWS, 128), I32),
             pltpu.VMEM((ROWS, 128), I32),
             pltpu.VMEM((4, CAP), I32),
@@ -363,12 +404,18 @@
             pltpu.VMEM((5, ROWS, 128), F32),
             pltpu.VMEM((6 * ROWS, 256), BF16),
             pltpu.VMEM((4, 8, CAP), F32),
+            pltpu.VMEM((5, 128, 256), F32),
+            pltpu.VMEM((3,) + cube, F32),
+            pltpu.VMEM(cube, F32),
+            pltpu.VMEM(cube, F32),
+            pltpu.VMEM((n_x + 8, n_y, n_z), F32),
+            pltpu.VMEM((n_x, n_y + 16, n_z), F32),
             pltpu.SemaphoreType.DMA((6,)),
             pltpu.SemaphoreType.DMA((8,)),
             pltpu.SemaphoreType.DMA((8,)),
         ],
         compiler_params=pltpu.CompilerParams(
-            collective_id=0, has_side_effects=True, vmem_limit_bytes=24 << 20
+            collective_id=0, has_side_effects=True, vmem_limit_bytes=36 << 20
         ),
         name="droplets",
     )(
@@ -386,32 +433,27 @@
         )
     )
     out, drops, cells = pl.pallas_call(
-        stencil_kernel,
-        grid=(1,),
+        edge_kernel,
         out_shape=(
-            shape((n_f, n_x, n_y, n_z)),
+            shape((n_f,) + cube),
             shape((5, SLOTS + 4 * CAP)),
             shape((ROWS + 8, 128), I32),
         ),
-        in_specs=[vmem] * 7,
-        out_specs=tuple(
-            pl.BlockSpec(s, lambda i, n=len(s): (0,) * n)
-            for s in ((n_f, n_x, n_y, n_z), (5, SLOTS + 4 * CAP), (ROWS + 8, 128))
-        ),
+        in_specs=[vmem] * 6,
+        out_specs=(hbm,) * 3,
         scratch_shapes=[
-            pltpu.VMEM((3, 16, 16, 128), F32),
-            pltpu.VMEM((16, 16, 128), F32),
-            pltpu.VMEM((16, 16, 128), F32),
-            pltpu.VMEM((2, 4, 16, 128), F32),
-            pltpu.VMEM((2, 4, 16, 128), F32),
-            pltpu.VMEM((16, 8, 128), F32),
-            pltpu.VMEM((16, 8, 128), F32),
-            pltpu.VMEM((24, 16, 128), F32),
-            pltpu.VMEM((16, 32, 128), F32),
+            pltpu.VMEM((n_f,) + cube, F32),
+            pltpu.VMEM((5, SLOTS + 4 * CAP), F32),
+            pltpu.VMEM((ROWS + 8, 128), I32),
+            pltpu.VMEM((2, 4, n_y, n_z), F32),
+            pltpu.VMEM((2, 4, n_y, n_z), F32),
+            pltpu.VMEM((n_x, 8, n_z), F32),
+            pltpu.VMEM((n_x, 8, n_z), F32),
+            pltpu.SemaphoreType.DMA((n_f + 2,)),
         ],
         compiler_params=pltpu.CompilerParams(vmem_limit_bytes=24 << 20),
-        name="stencil",
-    )(fv, xh, yh.reshape(n_f, n_x, 8, n_z), dep, own, own_cell, arr)
+        name="edges",
+    )(part, xh, yh.reshape(n_f, n_x, 8, n_z), own, own_cell, arr)
     return out, drops, cells.reshape(-1)
 
 

time: 40.3 us -> 29.6 us (0.73)
  the two profiles are of different devices: /device:TPU:96 before, /device:TPU:1 now
where the time goes in v2:
time: 29.6 us; the launch traced here: 29.5 us
  Pallas kernels  28.9 us (98%)
  between operations  0.64 us (2%)
    pallas_call x1, Pallas kernels, per_device(): pl.pallas_call(functools.partial(droplet_kernel, n_gx, n_gy), out_shape=(...  26.8 us
    pallas_call x1, Pallas kernels, per_device(): pl.pallas_call(edge_kernel, out_shape=(shape((n_f,) + cube), shape((5, SL...  2.06 us

profile of v2, /device:TPU:1, one launch (start us, length us, event | category | flops | bytes accessed | tf_op | source)
XLA Modules:
  0.0 29.5 jit_solution(963029696992742506)
XLA Ops:
  0.6 26.8 %droplets.1 = (f32[14,16,16,128]{3,2,1,0:T(8,128)S(1)}, f32[2,14,4,16,128]{4,3,2,1,0:T(8,128)S(1)}, f32[14,16,2,4,128]{4,3,2,1,0:T(4,128)S(1)}, f32[4,8,256]{2,1...) custom-call(f32[14,16,16,128]{3,2,1,0:T(8,128)} %fields.1, f32[14,16,4,4,128]{4,3,2,1,0:T(4,128)} %bitcast.6, ...), custom_call_target="tpu_custom_call" | custom-call | tf_op jit(solution)/shard_map/droplets/pallas_call | solution.py:382
  27.5 2.1 %edges.1 = (f32[14,16,16,128]{3,2,1,0:T(8,128)}, f32[5,9216]{1,0:T(8,128)}, s32[72,128]{1,0:T(8,128)}) custom-call(f32[14,16,16,128]{3,2,1,0:T(8,128)S(1)} %get-tuple-element.12.part, f32[2,14,4,16,128]{4,3,2,1,0:T(8,128)S(1)} %get-tuple-element.13.xh, f32[14,16,8,128]{3,2,1,0:T(8,128)S(1)} %bitcast.5, f32[5,8192]{1,0:T(8,128)S(1)} %get-tuple-element.15.own, ...), custom_call_target="tpu_custom_call" | custom-call | tf_op jit(solution)/shard_map/edges/pallas_call | solution.py:435

commit v3 on v2

--- a/solution.py
+++ b/solution.py
@@ -18,7 +18,7 @@
 SLOTS = 8192
 ROWS = SLOTS // 128
 CAP = 256
-TILE = 1024
+TILE = 2048
 
 
 def split(value):
@@ -53,7 +53,7 @@
     fields, fields_y, state, cell_h, new_cell_h, lists_h, counts_h,
     part, xh, yh, arr, own, own_cell,
     fv, cell, new_cell, lists, counts, st, table, s5, sv, gas, ns, msg, dep,
-    uv, pv, wv, fx, fy,
+    uv, pv, wv, tv, lv, fx, fy,
     in_sem, send_sem, recv_sem,
 ):
     gx = lax.axis_index("gx")
@@ -100,8 +100,8 @@
         )
         for i, (src, dst) in enumerate(faces)
     ]
-    for copy in sends:
-        copy.start()
+    for i in (2, 0, 3, 1):
+        sends[i].start()
     for copy in loads:
         copy.wait()
 
@@ -128,16 +128,28 @@
         sv[k] = high.astype(F32)
         sv[5 + k] = low.astype(F32)
 
+    def cell_step(x, carry):
+        q = [fv[f, x] for f in range(7)]
+        inverse, u, temper, p = primitives(q)
+        for a in range(3):
+            uv[a, x] = u[a]
+        pv[x] = p
+        tv[x] = temper
+        lv[x] = evap_log(temper, q[5], inverse)
+        wv[x] = 20.0 * q[5] * q[6] * inverse * jnp.exp(-2.0 / temper)
+        return carry
+
+    lax.fori_loop(0, 16, cell_step, 0, unroll=2)
+
     for h in range(2):
-        q = [fv[f, 8 * h : 8 * h + 8].reshape(128, 128) for f in range(6)]
-        inverse, u, temper, _ = primitives(q)
-        values = (u[0], u[1], u[2], temper, evap_log(temper, q[5], inverse))
+        values = [v[8 * h : 8 * h + 8].reshape(128, 128) for v in (uv.at[0], uv.at[1], uv.at[2], tv, lv)]
         for k, value in enumerate(values):
             high, low = split(value)
             table[k * 128 : (k + 1) * 128, h * 128 : h * 128 + 128] = high
             table[k * 128 : (k + 1) * 128, 256 + h * 128 : 384 + h * 128] = low
 
     per = TILE // 128
+    planes = 16 * per // ROWS
     column_ids = lax.broadcasted_iota(I32, (256, 128), 0)
     row_ids = lax.broadcasted_iota(I32, (128, 128), 0)
     dep[...] = jnp.zeros_like(dep)
@@ -179,6 +191,20 @@
         )
         for k in range(5):
             dep[k] += sums[k * 128 : (k + 1) * 128]
+        for i in range(planes):
+            x = t * planes + i
+            uz = uv[2, x]
+            p = pv[x]
+            for f in range(N_F):
+                fz = flux(f, 2, fv[f, x], uz, p)
+                total = None
+                for k in range(4):
+                    term = STENCIL[k] * (pltpu.roll(fz, 127 - k, 1) - pltpu.roll(fz, k + 1, 1))
+                    total = term if total is None else total + term
+                if SHARES[f] != 0.0:
+                    part[f, x] = SHARES[f] * wv[x] - total
+                else:
+                    part[f, x] = -total
         return carry
 
     lax.fori_loop(0, ROWS // per, droplet_step, 0)
@@ -242,26 +268,21 @@
         for k in range(5):
             own[k : k + 1, i * 128 : (i + 1) * 128] = gas[k, i : i + 1, :]
 
-    def cell_step(x, carry):
-        q = [fv[f, x] for f in range(7)]
-        inverse, u, temper, p = primitives(q)
-        for a in range(3):
-            uv[a, x] = u[a]
-        pv[x] = p
-        wv[x] = 20.0 * q[5] * q[6] * inverse * jnp.exp(-2.0 / temper)
-        log = evap_log(temper, q[5], inverse)
+    def deposit_step(x, carry):
+        u = [uv[a, x] for a in range(3)]
+        log = lv[x]
         rows = pl.ds(pl.multiple_of(lax.rem(x, 8) * 16, 16), 16)
         lanes = pl.ds(pl.multiple_of(lax.div(x, 8) * 128, 128), 128)
         sums = [dep[k, rows, lanes] for k in range(5)]
         evap = log * sums[0]
-        part[0, x] = evap
-        part[5, x] = evap
+        part[0, x] += evap
+        part[5, x] += evap
         for a in range(3):
-            part[1 + a, x] = (log + 0.8) * sums[1 + a] - 0.8 * u[a] * sums[0]
-        part[4, x] = (log + 0.6) * sums[4] - 0.6 * temper * sums[0]
+            part[1 + a, x] += (log + 0.8) * sums[1 + a] - 0.8 * u[a] * sums[0]
+        part[4, x] += (log + 0.6) * sums[4] - 0.6 * tv[x] * sums[0]
         return carry
 
-    lax.fori_loop(0, 16, cell_step, 0, unroll=2)
+    lax.fori_loop(0, 16, deposit_step, 0, unroll=2)
     blank = jnp.zeros((4, 16, 128), F32)
     fx[0:4] = blank
     fx[20:24] = blank
@@ -279,21 +300,13 @@
         lax.fori_loop(0, 16, flux_step, 0, unroll=8)
 
         def rate_step(x, carry):
-            fz = flux(f, 2, fv[f, x], uv[2, x], pv[x])
             total = None
             for k in range(4):
-                term = (
-                    (fx[x + 5 + k] - fx[x + 3 - k])
-                    + (fy[x, 9 + k : 25 + k] - fy[x, 7 - k : 23 - k])
-                    + (pltpu.roll(fz, 127 - k, 1) - pltpu.roll(fz, k + 1, 1))
+                term = (fx[x + 5 + k] - fx[x + 3 - k]) + (
+                    fy[x, 9 + k : 25 + k] - fy[x, 7 - k : 23 - k]
                 )
                 total = STENCIL[k] * term if total is None else total + STENCIL[k] * term
-            row = -total
-            if SHARES[f] != 0.0:
-                row = row + SHARES[f] * wv[x]
-            if f < 6:
-                row = row + part[f, x]
-            part[f, x] = row
+            part[f, x] -= total
             return carry
 
         lax.fori_loop(0, 16, rate_step, 0, unroll=8)
@@ -408,6 +421,8 @@
             pltpu.VMEM((3,) + cube, F32),
             pltpu.VMEM(cube, F32),
             pltpu.VMEM(cube, F32),
+            pltpu.VMEM(cube, F32),
+            pltpu.VMEM(cube, F32),
             pltpu.VMEM((n_x + 8, n_y, n_z), F32),
             pltpu.VMEM((n_x, n_y + 16, n_z), F32),
             pltpu.SemaphoreType.DMA((6,)),

time: 29.6 us -> 29 us (0.980)
  the two profiles are of different devices: /device:TPU:1 before, /device:TPU:0 now
where the time goes in v3:
time: 29 us; the launch traced here: 28.8 us
  Pallas kernels  28.2 us (97%)
  between operations  0.64 us (2%)
    pallas_call x1, Pallas kernels, per_device(): pl.pallas_call(functools.partial(droplet_kernel, n_gx, n_gy), out_shape=(...  26.1 us
    pallas_call x1, Pallas kernels, per_device(): pl.pallas_call(edge_kernel, out_shape=(shape((n_f,) + cube), shape((5, SL...  2.06 us

profile of v3, /device:TPU:0, one launch (start us, length us, event | category | flops | bytes accessed | tf_op | source)
XLA Modules:
  0.0 28.8 jit_solution(2657250005558082821)
XLA Ops:
  0.6 26.1 %droplets.1 = (f32[14,16,16,128]{3,2,1,0:T(8,128)S(1)}, f32[2,14,4,16,128]{4,3,2,1,0:T(8,128)S(1)}, f32[14,16,2,4,128]{4,3,2,1,0:T(4,128)S(1)}, f32[4,8,256]{2,1...) custom-call(f32[14,16,16,128]{3,2,1,0:T(8,128)} %fields.1, f32[14,16,4,4,128]{4,3,2,1,0:T(4,128)} %bitcast.6, ...), custom_call_target="tpu_custom_call" | custom-call | tf_op jit(solution)/shard_map/droplets/pallas_call | solution.py:395
  26.8 2.1 %edges.1 = (f32[14,16,16,128]{3,2,1,0:T(8,128)}, f32[5,9216]{1,0:T(8,128)}, s32[72,128]{1,0:T(8,128)}) custom-call(f32[14,16,16,128]{3,2,1,0:T(8,128)S(1)} %get-tuple-element.12.part, f32[2,14,4,16,128]{4,3,2,1,0:T(8,128)S(1)} %get-tuple-element.13.xh, f32[14,16,8,128]{3,2,1,0:T(8,128)S(1)} %bitcast.5, f32[5,8192]{1,0:T(8,128)S(1)} %get-tuple-element.15.own, ...), custom_call_target="tpu_custom_call" | custom-call | tf_op jit(solution)/shard_map/edges/pallas_call | solution.py:450

commit v4 on v3

--- a/solution.py
+++ b/solution.py
@@ -18,6 +18,7 @@
 SLOTS = 8192
 ROWS = SLOTS // 128
 CAP = 256
+FIRST = 7
 TILE = 2048
 
 
@@ -37,6 +38,28 @@
 
 def evap_log(temper, q5, inverse):
     return 0.5 * jnp.log(1.0 + temper / (1.0 + q5 * inverse))
+
+
+def cube_root(mass):
+    return jnp.exp(jnp.log(mass) * (1.0 / 3.0))
+
+
+def cell_place(c):
+    column = lax.shift_left(lax.shift_right_logical(c, 14), 7) + (c & 127)
+    return column, lax.shift_right_logical(c, 7) & 127
+
+
+def advance(mass, theta, v, around, size):
+    inverse = 1.0 / mass
+    evap = size * around[4]
+    heat = 0.6 * size * (around[3] - theta)
+    result = [
+        mass - 0.05 * evap,
+        theta + 0.05 * (heat - 0.3 * evap) * inverse,
+    ]
+    for a in range(3):
+        result.append(v[a] + 0.04 * size * (around[a] - v[a]) * inverse)
+    return result
 
 
 def flux(f, axis, value, u, p):
@@ -81,27 +104,39 @@
     ]
     for copy in loads:
         copy.start()
-    pl.semaphore_wait(barrier, 4)
     n_x = fields.shape[1]
-    faces = (
-        (fields.at[:, n_x - 4 : n_x], xh.at[0]),
-        (fields.at[:, 0:4], xh.at[1]),
-        (fields_y.at[:, :, 3], yh.at[:, :, 1]),
-        (fields_y.at[:, :, 0], yh.at[:, :, 0]),
-    )
-    sends = [
-        pltpu.make_async_remote_copy(
-            src_ref=src,
-            dst_ref=dst,
-            send_sem=send_sem.at[i],
-            recv_sem=recv_sem.at[i],
-            device_id=targets[i],
-            device_id_type=MESH,
-        )
-        for i, (src, dst) in enumerate(faces)
-    ]
-    for i in (2, 0, 3, 1):
-        sends[i].start()
+    sends = []
+    for i, part_of in enumerate((slice(0, FIRST), slice(FIRST, N_F))):
+        faces = (
+            (fields.at[part_of, n_x - 4 : n_x], xh.at[0, part_of]),
+            (fields.at[part_of, 0:4], xh.at[1, part_of]),
+            (fields_y.at[part_of, :, 3], yh.at[part_of, :, 1]),
+            (fields_y.at[part_of, :, 0], yh.at[part_of, :, 0]),
+        )
+        for j, (src, dst) in enumerate(faces):
+            sends.append(
+                pltpu.make_async_remote_copy(
+                    src_ref=src,
+                    dst_ref=dst,
+                    send_sem=send_sem.at[4 * i + j],
+                    recv_sem=recv_sem.at[4 * i + j],
+                    device_id=targets[j],
+                    device_id_type=MESH,
+                )
+            )
+    def send_faces(first):
+        y_low = lax.rem(gy, 8) == 0
+        x_low = lax.rem(gx, 4) == 0
+        for low, i, j in ((y_low, 3, 2), (x_low, 1, 0), (y_low, 2, 3), (x_low, 0, 1)):
+            pl.when(low)(sends[first + i].start)
+            pl.when(jnp.logical_not(low))(sends[first + j].start)
+
+    def meet_and_send():
+        pl.semaphore_wait(barrier, 4)
+        send_faces(0)
+
+    first_plane = lax.rem(gx, 4) == 0
+    pl.when(jnp.logical_not(first_plane))(meet_and_send)
     for copy in loads:
         copy.wait()
 
@@ -114,7 +149,7 @@
     live = slot < counts[0:1, 0:1]
     mass = s5[0]
     theta = s5[1]
-    size = jnp.exp(jnp.log(mass) * (1.0 / 3.0))
+    size = cube_root(mass)
     live_size = jnp.where(live, size, 0.0)
     weights = (
         live_size,
@@ -148,6 +183,72 @@
             table[k * 128 : (k + 1) * 128, h * 128 : h * 128 + 128] = high
             table[k * 128 : (k + 1) * 128, 256 + h * 128 : 384 + h * 128] = low
 
+    pl.when(first_plane)(meet_and_send)
+
+    def place(values, row):
+        high, low = values
+        ns[row * ROWS : (row + 1) * ROWS, 0:128] = high
+        ns[row * ROWS : (row + 1) * ROWS, 128:256] = low
+
+    for k in range(5):
+        place(split(s5[k]), k)
+    for k, ids in ((5, new_cell[...]), (6, cell[...])):
+        upper = lax.shift_left(lax.shift_right_logical(ids, 8), 8)
+        place((upper.astype(F32).astype(BF16), (ids & 255).astype(F32).astype(BF16)), k)
+    entry = lax.broadcasted_iota(I32, (1, CAP), 1)
+    slot_rows = lax.broadcasted_iota(I32, (ROWS, CAP), 0)
+    slot_lanes = lax.broadcasted_iota(I32, (128, CAP), 0)
+    wide_columns = lax.broadcasted_iota(I32, (256, CAP), 0)
+    wide_rows = lax.broadcasted_iota(I32, (128, CAP), 0)
+    departed = jnp.zeros((ROWS, 128), F32)
+    for r in range(4):
+        picked = lists[r : r + 1, :]
+        valid = entry < counts[0:1, 1 + r : 2 + r]
+        row_mask = slot_rows == lax.shift_right_logical(picked, 7)
+        lane_hot = jnp.where(slot_lanes == (picked & 127), 1.0, 0.0).astype(BF16)
+        row_hot = jnp.where(row_mask & valid, 1.0, 0.0).astype(BF16)
+        departed += lax.dot_general(
+            row_hot, lane_hot, (((1,), (1,)), ((), ())), preferred_element_type=F32
+        )
+        rows = jnp.dot(
+            ns[...], jnp.concatenate([lane_hot, lane_hot], 0), preferred_element_type=F32
+        )
+        got = [
+            jnp.sum(
+                jnp.where(row_mask, rows[k * ROWS : (k + 1) * ROWS], 0.0), axis=0, keepdims=True
+            )
+            for k in range(7)
+        ]
+        column, row = cell_place(got[6].astype(I32))
+        hot = jnp.where(wide_columns == column, 1.0, 0.0).astype(BF16)
+        rows = jnp.dot(
+            table[...], jnp.concatenate([hot, hot], 0), preferred_element_type=F32
+        )
+        around = [
+            jnp.sum(
+                jnp.where(wide_rows == row, rows[k * 128 : (k + 1) * 128], 0.0),
+                axis=0,
+                keepdims=True,
+            )
+            for k in range(5)
+        ]
+        moved = advance(got[0], got[1], got[2:5], around, cube_root(got[0]))
+        for k in range(5):
+            msg[r, k : k + 1, :] = jnp.where(valid, moved[k], 0.0)
+        msg[r, 5:6, :] = jnp.where(valid, got[5], -1.0)
+        msg[r, 6:8, :] = jnp.zeros((2, CAP), F32)
+        copy = pltpu.make_async_remote_copy(
+            src_ref=msg.at[r],
+            dst_ref=arr.at[r],
+            send_sem=send_sem.at[8 + r],
+            recv_sem=recv_sem.at[8 + r],
+            device_id=targets[r],
+            device_id_type=MESH,
+        )
+        copy.start()
+        sends.append(copy)
+    send_faces(4)
+
     per = TILE // 128
     planes = 16 * per // ROWS
     column_ids = lax.broadcasted_iota(I32, (256, 128), 0)
@@ -159,8 +260,7 @@
         masks = []
         for j in range(per):
             c = cell[pl.ds(t * per + j, 1), :]
-            column = lax.shift_left(lax.shift_right_logical(c, 14), 7) + (c & 127)
-            row = lax.shift_right_logical(c, 7) & 127
+            column, row = cell_place(c)
             hots.append(jnp.where(column_ids == column, 1.0, 0.0).astype(BF16))
             masks.append(row_ids == row)
         for j in range(0, per, 2):
@@ -209,59 +309,9 @@
 
     lax.fori_loop(0, ROWS // per, droplet_step, 0)
 
-    inv_mass = 1.0 / mass
-    evap = size * gas[4]
-    heat = 0.6 * size * (gas[3] - theta)
-    new_state = [
-        mass - 0.05 * evap,
-        theta + 0.05 * (heat - 0.3 * evap) * inv_mass,
-    ]
-    for a in range(3):
-        v = s5[2 + a]
-        new_state.append(v + 0.04 * size * (gas[a] - v) * inv_mass)
-    for k in range(5):
-        high, low = split(new_state[k])
-        ns[k * ROWS : (k + 1) * ROWS, 0:128] = high
-        ns[k * ROWS : (k + 1) * ROWS, 128:256] = low
-    cells = new_cell[...]
-    cell_high = lax.shift_left(lax.shift_right_logical(cells, 8), 8)
-    ns[5 * ROWS : 6 * ROWS, 0:128] = cell_high.astype(F32).astype(BF16)
-    ns[5 * ROWS : 6 * ROWS, 128:256] = (cells & 255).astype(F32).astype(BF16)
-
-    entry = lax.broadcasted_iota(I32, (1, CAP), 1)
-    slot_rows = lax.broadcasted_iota(I32, (ROWS, CAP), 0)
-    slot_lanes = lax.broadcasted_iota(I32, (128, CAP), 0)
-    departed = jnp.zeros((ROWS, 128), F32)
-    for r in range(4):
-        picked = lists[r : r + 1, :]
-        valid = entry < counts[0:1, 1 + r : 2 + r]
-        row_mask = slot_rows == lax.shift_right_logical(picked, 7)
-        lane_hot = jnp.where(slot_lanes == (picked & 127), 1.0, 0.0).astype(BF16)
-        row_hot = jnp.where(row_mask & valid, 1.0, 0.0).astype(BF16)
-        departed += lax.dot_general(
-            row_hot, lane_hot, (((1,), (1,)), ((), ())), preferred_element_type=F32
-        )
-        rows = jnp.dot(
-            ns[...], jnp.concatenate([lane_hot, lane_hot], 0), preferred_element_type=F32
-        )
-        for k in range(6):
-            got = jnp.sum(
-                jnp.where(row_mask, rows[k * ROWS : (k + 1) * ROWS], 0.0), axis=0, keepdims=True
-            )
-            msg[r, k : k + 1, :] = jnp.where(valid, got, 0.0 if k < 5 else -1.0)
-        msg[r, 6:8, :] = jnp.zeros((2, CAP), F32)
-        copy = pltpu.make_async_remote_copy(
-            src_ref=msg.at[r],
-            dst_ref=arr.at[r],
-            send_sem=send_sem.at[4 + r],
-            recv_sem=recv_sem.at[4 + r],
-            device_id=targets[r],
-            device_id_type=MESH,
-        )
-        copy.start()
-        sends.append(copy)
+    new_state = advance(mass, theta, [s5[2], s5[3], s5[4]], [gas[k] for k in range(5)], size)
     staying = live & (departed == 0.0)
-    own_cell[...] = jnp.where(staying, cells, -1)
+    own_cell[...] = jnp.where(staying, new_cell[...], -1)
     for k in range(5):
         gas[k] = jnp.where(staying, new_state[k], 0.0)
     for i in range(ROWS):
@@ -415,7 +465,7 @@
             pltpu.VMEM((5, ROWS, 128), F32),
             pltpu.VMEM((10, ROWS, 128), F32),
             pltpu.VMEM((5, ROWS, 128), F32),
-            pltpu.VMEM((6 * ROWS, 256), BF16),
+            pltpu.VMEM((7 * ROWS, 256), BF16),
             pltpu.VMEM((4, 8, CAP), F32),
             pltpu.VMEM((5, 128, 256), F32),
             pltpu.VMEM((3,) + cube, F32),
@@ -426,8 +476,8 @@
             pltpu.VMEM((n_x + 8, n_y, n_z), F32),
             pltpu.VMEM((n_x, n_y + 16, n_z), F32),
             pltpu.SemaphoreType.DMA((6,)),
-            pltpu.SemaphoreType.DMA((8,)),
-            pltpu.SemaphoreType.DMA((8,)),
+            pltpu.SemaphoreType.DMA((12,)),
+            pltpu.SemaphoreType.DMA((12,)),
         ],
         compiler_params=pltpu.CompilerParams(
             collective_id=0, has_side_effects=True, vmem_limit_bytes=36 << 20

time: 29 us -> 26.6 us (0.917)
  the two profiles are of different devices: /device:TPU:0 before, /device:TPU:96 now
where the time goes in v4:
time: 26.6 us; the launch traced here: 26.2 us
  Pallas kernels  25.5 us (96%)
  between operations  0.64 us (2%)
    pallas_call x1, Pallas kernels, per_device(): pl.pallas_call(functools.partial(droplet_kernel, n_gx, n_gy), out_shape=(...  23.5 us
    pallas_call x1, Pallas kernels, per_device(): pl.pallas_call(edge_kernel, out_shape=(shape((n_f,) + cube), shape((5, SL...  2.06 us

profile of v4, /device:TPU:96, one launch (start us, length us, event | category | flops | bytes accessed | tf_op | source)
XLA Modules:
  0.0 26.2 jit_solution(8486509806231102731)
XLA Ops:
  0.6 23.5 %droplets.1 = (f32[14,16,16,128]{3,2,1,0:T(8,128)S(1)}, f32[2,14,4,16,128]{4,3,2,1,0:T(8,128)S(1)}, f32[14,16,2,4,128]{4,3,2,1,0:T(4,128)S(1)}, f32[4,8,256]{2,1...) custom-call(f32[14,16,16,128]{3,2,1,0:T(8,128)} %fields.1, f32[14,16,4,4,128]{4,3,2,1,0:T(4,128)} %bitcast.6, ...), custom_call_target="tpu_custom_call" | custom-call | tf_op jit(solution)/shard_map/droplets/pallas_call | solution.py:445
  24.1 2.1 %edges.1 = (f32[14,16,16,128]{3,2,1,0:T(8,128)}, f32[5,9216]{1,0:T(8,128)}, s32[72,128]{1,0:T(8,128)}) custom-call(f32[14,16,16,128]{3,2,1,0:T(8,128)S(1)} %get-tuple-element.12.part, f32[2,14,4,16,128]{4,3,2,1,0:T(8,128)S(1)} %get-tuple-element.13.xh, f32[14,16,8,128]{3,2,1,0:T(8,128)S(1)} %bitcast.5, f32[5,8192]{1,0:T(8,128)S(1)} %get-tuple-element.15.own, ...), custom_call_target="tpu_custom_call" | custom-call | tf_op jit(solution)/shard_map/edges/pallas_call | solution.py:500

commit v5 on v4

--- a/solution.py
+++ b/solution.py
@@ -74,8 +74,8 @@
 def droplet_kernel(
     n_gx, n_gy,
     fields, fields_y, state, cell_h, new_cell_h, lists_h, counts_h,
-    part, xh, yh, arr, own, own_cell,
-    fv, cell, new_cell, lists, counts, st, table, s5, sv, gas, ns, msg, dep,
+    part, xh, yh, drops, cells,
+    fv, cell, new_cell, lists, counts, st, table, s5, sv, gas, ns, msg, arr, dep,
     uv, pv, wv, tv, lv, fx, fy,
     in_sem, send_sem, recv_sem,
 ):
@@ -124,20 +124,33 @@
                     device_id_type=MESH,
                 )
             )
-    def send_faces(first):
-        y_low = lax.rem(gy, 8) == 0
-        x_low = lax.rem(gx, 4) == 0
-        for low, i, j in ((y_low, 3, 2), (x_low, 1, 0), (y_low, 2, 3), (x_low, 0, 1)):
-            pl.when(low)(sends[first + i].start)
-            pl.when(jnp.logical_not(low))(sends[first + j].start)
+    plane = lax.rem(gx, 4)
+    y_low = lax.rem(gy, 8) == 0
+
+    def send_faces(batch):
+        for y_first, y_second, y_is in ((3, 2, y_low), (2, 3, jnp.logical_not(y_low))):
+            orders = (
+                (plane == 0, ((y_first, y_first + 4, 0), (1, 5, y_second, y_second + 4, 4))),
+                (plane == 3, ((0, 4, 1), (y_first, y_first + 4, y_second, y_second + 4, 5))),
+                (
+                    (plane == 1) | (plane == 2),
+                    ((y_first, 0, y_second, 1), (y_first + 4, 4, y_second + 4, 5)),
+                ),
+            )
+            for here, batches in orders:
+
+                @pl.when(here & y_is)
+                def _(batches=batches):
+                    for i in batches[batch]:
+                        sends[i].start()
 
     def meet_and_send():
         pl.semaphore_wait(barrier, 4)
         send_faces(0)
 
-    first_plane = lax.rem(gx, 4) == 0
+    first_plane = plane == 0
     pl.when(jnp.logical_not(first_plane))(meet_and_send)
-    for copy in loads:
+    for copy in loads[:5]:
         copy.wait()
 
     for i in range(ROWS):
@@ -163,6 +176,8 @@
         sv[k] = high.astype(F32)
         sv[5 + k] = low.astype(F32)
 
+    loads[5].wait()
+
     def cell_step(x, carry):
         q = [fv[f, x] for f in range(7)]
         inverse, u, temper, p = primitives(q)
@@ -172,10 +187,18 @@
         tv[x] = temper
         lv[x] = evap_log(temper, q[5], inverse)
         wv[x] = 20.0 * q[5] * q[6] * inverse * jnp.exp(-2.0 / temper)
+        for f in range(N_F):
+            fx[f, x + 4] = flux(f, 0, fv[f, x], u[0], p)
         return carry
 
+    for f in range(N_F):
+        fx[f, 0:4] = jnp.zeros((4, 16, 128), F32)
+        fx[f, 20:24] = jnp.zeros((4, 16, 128), F32)
+        for i in range(fy.shape[1]):
+            fy[f, i, 0:8] = jnp.zeros((8, 128), F32)
+            fy[f, i, 24:32] = jnp.zeros((8, 128), F32)
+
     lax.fori_loop(0, 16, cell_step, 0, unroll=2)
-
     for h in range(2):
         values = [v[8 * h : 8 * h + 8].reshape(128, 128) for v in (uv.at[0], uv.at[1], uv.at[2], tv, lv)]
         for k, value in enumerate(values):
@@ -195,47 +218,39 @@
     for k, ids in ((5, new_cell[...]), (6, cell[...])):
         upper = lax.shift_left(lax.shift_right_logical(ids, 8), 8)
         place((upper.astype(F32).astype(BF16), (ids & 255).astype(F32).astype(BF16)), k)
+    leaving = 4 * CAP
     entry = lax.broadcasted_iota(I32, (1, CAP), 1)
-    slot_rows = lax.broadcasted_iota(I32, (ROWS, CAP), 0)
-    slot_lanes = lax.broadcasted_iota(I32, (128, CAP), 0)
-    wide_columns = lax.broadcasted_iota(I32, (256, CAP), 0)
-    wide_rows = lax.broadcasted_iota(I32, (128, CAP), 0)
-    departed = jnp.zeros((ROWS, 128), F32)
+    picked = jnp.concatenate([lists[r : r + 1, :] for r in range(4)], 1)
+    valid = [entry < counts[0:1, 1 + r : 2 + r] for r in range(4)]
+    row_mask = lax.broadcasted_iota(I32, (ROWS, leaving), 0) == lax.shift_right_logical(picked, 7)
+    lane_hot = jnp.where(
+        lax.broadcasted_iota(I32, (128, leaving), 0) == (picked & 127), 1.0, 0.0
+    ).astype(BF16)
+    row_hot = jnp.where(row_mask & jnp.concatenate(valid, 1), 1.0, 0.0).astype(BF16)
+    departed = lax.dot_general(
+        row_hot, lane_hot, (((1,), (1,)), ((), ())), preferred_element_type=F32
+    )
+    rows = jnp.dot(ns[...], jnp.concatenate([lane_hot, lane_hot], 0), preferred_element_type=F32)
+    got = [
+        jnp.sum(jnp.where(row_mask, rows[k * ROWS : (k + 1) * ROWS], 0.0), axis=0, keepdims=True)
+        for k in range(7)
+    ]
+    column, row = cell_place(got[6].astype(I32))
+    hot = jnp.where(
+        lax.broadcasted_iota(I32, (256, leaving), 0) == column, 1.0, 0.0
+    ).astype(BF16)
+    rows = jnp.dot(table[...], jnp.concatenate([hot, hot], 0), preferred_element_type=F32)
+    row_mask = lax.broadcasted_iota(I32, (128, leaving), 0) == row
+    around = [
+        jnp.sum(jnp.where(row_mask, rows[k * 128 : (k + 1) * 128], 0.0), axis=0, keepdims=True)
+        for k in range(5)
+    ]
+    moved = advance(got[0], got[1], got[2:5], around, cube_root(got[0]))
     for r in range(4):
-        picked = lists[r : r + 1, :]
-        valid = entry < counts[0:1, 1 + r : 2 + r]
-        row_mask = slot_rows == lax.shift_right_logical(picked, 7)
-        lane_hot = jnp.where(slot_lanes == (picked & 127), 1.0, 0.0).astype(BF16)
-        row_hot = jnp.where(row_mask & valid, 1.0, 0.0).astype(BF16)
-        departed += lax.dot_general(
-            row_hot, lane_hot, (((1,), (1,)), ((), ())), preferred_element_type=F32
-        )
-        rows = jnp.dot(
-            ns[...], jnp.concatenate([lane_hot, lane_hot], 0), preferred_element_type=F32
-        )
-        got = [
-            jnp.sum(
-                jnp.where(row_mask, rows[k * ROWS : (k + 1) * ROWS], 0.0), axis=0, keepdims=True
-            )
-            for k in range(7)
-        ]
-        column, row = cell_place(got[6].astype(I32))
-        hot = jnp.where(wide_columns == column, 1.0, 0.0).astype(BF16)
-        rows = jnp.dot(
-            table[...], jnp.concatenate([hot, hot], 0), preferred_element_type=F32
-        )
-        around = [
-            jnp.sum(
-                jnp.where(wide_rows == row, rows[k * 128 : (k + 1) * 128], 0.0),
-                axis=0,
-                keepdims=True,
-            )
-            for k in range(5)
-        ]
-        moved = advance(got[0], got[1], got[2:5], around, cube_root(got[0]))
+        lanes = slice(r * CAP, (r + 1) * CAP)
         for k in range(5):
-            msg[r, k : k + 1, :] = jnp.where(valid, moved[k], 0.0)
-        msg[r, 5:6, :] = jnp.where(valid, got[5], -1.0)
+            msg[r, k : k + 1, :] = jnp.where(valid[r], moved[k][:, lanes], 0.0)
+        msg[r, 5:6, :] = jnp.where(valid[r], got[5][:, lanes], -1.0)
         msg[r, 6:8, :] = jnp.zeros((2, CAP), F32)
         copy = pltpu.make_async_remote_copy(
             src_ref=msg.at[r],
@@ -247,7 +262,7 @@
         )
         copy.start()
         sends.append(copy)
-    send_faces(4)
+    send_faces(1)
 
     per = TILE // 128
     planes = 16 * per // ROWS
@@ -293,13 +308,20 @@
             dep[k] += sums[k * 128 : (k + 1) * 128]
         for i in range(planes):
             x = t * planes + i
+            uy = uv[1, x]
             uz = uv[2, x]
             p = pv[x]
             for f in range(N_F):
-                fz = flux(f, 2, fv[f, x], uz, p)
+                value = fv[f, x]
+                fy[f, i, 8:24] = flux(f, 1, value, uy, p)
+                fz = flux(f, 2, value, uz, p)
                 total = None
                 for k in range(4):
-                    term = STENCIL[k] * (pltpu.roll(fz, 127 - k, 1) - pltpu.roll(fz, k + 1, 1))
+                    term = STENCIL[k] * (
+                        (fx[f, x + 5 + k] - fx[f, x + 3 - k])
+                        + (fy[f, i, 9 + k : 25 + k] - fy[f, i, 7 - k : 23 - k])
+                        + (pltpu.roll(fz, 127 - k, 1) - pltpu.roll(fz, k + 1, 1))
+                    )
                     total = term if total is None else total + term
                 if SHARES[f] != 0.0:
                     part[f, x] = SHARES[f] * wv[x] - total
@@ -311,12 +333,12 @@
 
     new_state = advance(mass, theta, [s5[2], s5[3], s5[4]], [gas[k] for k in range(5)], size)
     staying = live & (departed == 0.0)
-    own_cell[...] = jnp.where(staying, new_cell[...], -1)
+    cells[0:ROWS, :] = jnp.where(staying, new_cell[...], -1)
     for k in range(5):
         gas[k] = jnp.where(staying, new_state[k], 0.0)
     for i in range(ROWS):
         for k in range(5):
-            own[k : k + 1, i * 128 : (i + 1) * 128] = gas[k, i : i + 1, :]
+            drops[k : k + 1, i * 128 : (i + 1) * 128] = gas[k, i : i + 1, :]
 
     def deposit_step(x, carry):
         u = [uv[a, x] for a in range(3)]
@@ -333,49 +355,22 @@
         return carry
 
     lax.fori_loop(0, 16, deposit_step, 0, unroll=2)
-    blank = jnp.zeros((4, 16, 128), F32)
-    fx[0:4] = blank
-    fx[20:24] = blank
-    for x in range(16):
-        fy[x, 0:8] = jnp.zeros((8, 128), F32)
-        fy[x, 24:32] = jnp.zeros((8, 128), F32)
-    for f in range(N_F):
-
-        def flux_step(x, carry):
-            value = fv[f, x]
-            fx[4 + x] = flux(f, 0, value, uv[0, x], pv[x])
-            fy[x, 8:24] = flux(f, 1, value, uv[1, x], pv[x])
-            return carry
-
-        lax.fori_loop(0, 16, flux_step, 0, unroll=8)
-
-        def rate_step(x, carry):
-            total = None
-            for k in range(4):
-                term = (fx[x + 5 + k] - fx[x + 3 - k]) + (
-                    fy[x, 9 + k : 25 + k] - fy[x, 7 - k : 23 - k]
-                )
-                total = STENCIL[k] * term if total is None else total + STENCIL[k] * term
-            part[f, x] -= total
-            return carry
-
-        lax.fori_loop(0, 16, rate_step, 0, unroll=8)
-    for copy in sends:
+    for copy in sends[8:]:
         copy.wait()
-
-
-def edge_kernel(
-    part, xh, yh, own, own_cell, arr,
-    out_h, drops_h, cells_h,
-    out, drops, cells, ux, px, uy, py, sem,
-):
-    drops[:, 0:SLOTS] = own[...]
-    cells[0:ROWS, :] = own_cell[...]
     for r in range(4):
         drops[:, SLOTS + CAP * r : SLOTS + CAP * (r + 1)] = arr[r, 0:5, :]
         for j in range(2):
             row = ROWS + 2 * r + j
             cells[row : row + 1, :] = arr[r, 5:6, 128 * j : 128 * j + 128].astype(I32)
+    for copy in sends[:8]:
+        copy.wait()
+
+
+def edge_kernel(
+    part, xh, yh, drops, cells,
+    out_h, drops_h, cells_h,
+    out, ux, px, uy, py, sem,
+):
     copies = [
         pltpu.make_async_copy(drops, drops_h, sem.at[N_F]),
         pltpu.make_async_copy(cells, cells_h, sem.at[N_F + 1]),
@@ -442,18 +437,17 @@
     vmem = pl.BlockSpec(memory_space=pltpu.VMEM)
     hbm = pl.BlockSpec(memory_space=pltpu.HBM)
     cube = (n_x, n_y, n_z)
-    part, xh, yh, arr, own, own_cell = pl.pallas_call(
+    part, xh, yh, drops, cells = pl.pallas_call(
         functools.partial(droplet_kernel, n_gx, n_gy),
         out_shape=(
             shape((n_f,) + cube),
             shape((2, n_f, 4, n_y, n_z)),
             shape((n_f, n_x, 2, 4, n_z)),
-            shape((4, 8, CAP)),
-            shape((5, SLOTS)),
-            shape((ROWS, 128), I32),
+            shape((5, SLOTS + 4 * CAP)),
+            shape((ROWS + 8, 128), I32),
         ),
         in_specs=[hbm] * 7,
-        out_specs=(vmem,) * 6,
+        out_specs=(vmem,) * 5,
         scratch_shapes=[
             pltpu.VMEM((n_f,) + cube, F32),
             pltpu.VMEM((ROWS, 128), I32),
@@ -467,14 +461,15 @@
             pltpu.VMEM((5, ROWS, 128), F32),
             pltpu.VMEM((7 * ROWS, 256), BF16),
             pltpu.VMEM((4, 8, CAP), F32),
+            pltpu.VMEM((4, 8, CAP), F32),
             pltpu.VMEM((5, 128, 256), F32),
             pltpu.VMEM((3,) + cube, F32),
             pltpu.VMEM(cube, F32),
             pltpu.VMEM(cube, F32),
             pltpu.VMEM(cube, F32),
             pltpu.VMEM(cube, F32),
-            pltpu.VMEM((n_x + 8, n_y, n_z), F32),
-            pltpu.VMEM((n_x, n_y + 16, n_z), F32),
+            pltpu.VMEM((n_f, n_x + 8, n_y, n_z), F32),
+            pltpu.VMEM((n_f, n_x * TILE // SLOTS, n_y + 16, n_z), F32),
             pltpu.SemaphoreType.DMA((6,)),
             pltpu.SemaphoreType.DMA((12,)),
             pltpu.SemaphoreType.DMA((12,)),
@@ -504,12 +499,10 @@
             shape((5, SLOTS + 4 * CAP)),
             shape((ROWS + 8, 128), I32),
         ),
-        in_specs=[vmem] * 6,
+        in_specs=[vmem] * 5,
         out_specs=(hbm,) * 3,
         scratch_shapes=[
             pltpu.VMEM((n_f,) + cube, F32),
-            pltpu.VMEM((5, SLOTS + 4 * CAP), F32),
-            pltpu.VMEM((ROWS + 8, 128), I32),
             pltpu.VMEM((2, 4, n_y, n_z), F32),
             pltpu.VMEM((2, 4, n_y, n_z), F32),
             pltpu.VMEM((n_x, 8, n_z), F32),
@@ -518,7 +511,7 @@
         ],
         compiler_params=pltpu.CompilerParams(vmem_limit_bytes=24 << 20),
         name="edges",
-    )(part, xh, yh.reshape(n_f, n_x, 8, n_z), own, own_cell, arr)
+    )(part, xh, yh.reshape(n_f, n_x, 8, n_z), drops, cells)
     return out, drops, cells.reshape(-1)
 
 

time: 26.6 us -> 25.2 us (0.947); the launches traced: 26.2 us -> 25.1 us
  Pallas kernels: 25.5 us -> 24.5 us
    pallas_call x1, Pallas kernels: 23.5 us -> 22.4 us  [per_device(): pl.pallas_call(functools.partial(droplet_kernel, n_gx, n_gy), out_shape=(...]
where the time goes in v5:
time: 25.2 us; the launch traced here: 25.1 us
  Pallas kernels  24.5 us (97%)
  between operations  0.64 us (3%)
    pallas_call x1, Pallas kernels, per_device(): pl.pallas_call(functools.partial(droplet_kernel, n_gx, n_gy), out_shape=(...  22.4 us
    pallas_call x1, Pallas kernels, per_device(): pl.pallas_call(edge_kernel, out_shape=(shape((n_f,) + cube), shape((5, SL...  2.03 us

profile of v5, /device:TPU:96, one launch (start us, length us, event | category | flops | bytes accessed | tf_op | source)
XLA Modules:
  0.0 25.1 jit_solution(6959430241746521230)
XLA Ops:
  0.6 22.4 %droplets.1 = (f32[14,16,16,128]{3,2,1,0:T(8,128)S(1)}, f32[2,14,4,16,128]{4,3,2,1,0:T(8,128)S(1)}, f32[14,16,2,4,128]{4,3,2,1,0:T(4,128)S(1)}, f32[5,9216]{1,0:T(8,128)S(1)}, s32[72,128]{1,0:T(8,128)S(1)}) custom-call(f32[14,16,16,128]{3,2,1,0:T(8,128)} %fields.1, f32[14,16,4,4,128]{4,3,2,1,0:T(4,128)} %bitcast.6, f32[5,8192]{1,0:T(8,128)} %state.1, ...), custom_call_target="tpu_custom_call" | custom-call | tf_op jit(solution)/shard_map/droplets/pallas_call | solution.py:440
  23.1 2.0 %edges.1 = (f32[14,16,16,128]{3,2,1,0:T(8,128)}, f32[5,9216]{1,0:T(8,128)}, s32[72,128]{1,0:T(8,128)}) custom-call(f32[14,16,16,128]{3,2,1,0:T(8,128)S(1)} %get-tuple-element.11.part, f32[2,14,4,16,128]{4,3,2,1,0:T(8,128)S(1)} %get-tuple-element.12.xh, f32[14,16,8,128]{3,2,1,0:T(8,128)S(1)} %bitcast.5, f32[5,9216]{1,0:T(8,128)S(1)} %get-tuple-element.14.drops, ...), custom_call_target="tpu_custom_call" | custom-call | tf_op jit(solution)/shard_map/edges/pallas_call | solution.py:495

commit v6 on v5

--- a/solution.py
+++ b/solution.py
@@ -369,7 +369,7 @@
 def edge_kernel(
     part, xh, yh, drops, cells,
     out_h, drops_h, cells_h,
-    out, ux, px, uy, py, sem,
+    out, ux, px, uy, py, fy, sem,
 ):
     copies = [
         pltpu.make_async_copy(drops, drops_h, sem.at[N_F]),
@@ -384,30 +384,33 @@
         py[x] = p
         return carry
 
-    lax.fori_loop(0, 16, cell_step, 0, unroll=4)
+    lax.fori_loop(0, 16, cell_step, 0, unroll=16)
     for s in range(2):
         for i in range(4):
             _, u, _, p = primitives([xh[s, f, i] for f in range(5)])
             ux[s, i] = u[0]
             px[s, i] = p
 
-    row = lax.broadcasted_iota(I32, (8, 128), 0)
-    zero = jnp.zeros((8, 128), F32)
-    down = [jnp.where(row < k + 1, -STENCIL[k], 0.0) for k in range(4)]
-    up = [jnp.where(row >= 7 - k, STENCIL[k], 0.0) for k in range(4)]
+    for x in range(16):
+        fy[x, 8:24] = jnp.zeros((16, 128), F32)
     for f in range(N_F):
 
         def y_step(x, carry):
             edge = flux(f, 1, yh[f, x], uy[x], py[x])
-            total = (down[3] + up[3]) * pltpu.roll(edge, 4, 0)
-            for k in range(3):
-                total = total + down[k] * pltpu.roll(edge, k + 1, 0)
-                total = total + up[k] * pltpu.roll(edge, 7 - k, 0)
-            out[f, x, 0:8] = part[f, x, 0:8] - jnp.where(row < 4, total, zero)
-            out[f, x, 8:16] = part[f, x, 8:16] - jnp.where(row < 4, zero, total)
+            fy[x, 0:8] = edge
+            fy[x, 24:32] = edge
+            low = None
+            high = None
+            for k in range(4):
+                term = STENCIL[k] * fy[x, 7 - k : 15 - k]
+                low = term if low is None else low + term
+                term = STENCIL[k] * fy[x, 17 + k : 25 + k]
+                high = term if high is None else high + term
+            out[f, x, 0:8] = part[f, x, 0:8] + low
+            out[f, x, 8:16] = part[f, x, 8:16] - high
             return carry
 
-        lax.fori_loop(0, 16, y_step, 0, unroll=8)
+        lax.fori_loop(0, 16, y_step, 0, unroll=16)
         low = [flux(f, 0, xh[0, f, i], ux[0, i], px[0, i]) for i in range(4)]
         high = [flux(f, 0, xh[1, f, i], ux[1, i], px[1, i]) for i in range(4)]
         for x in range(4):
@@ -507,6 +510,7 @@
             pltpu.VMEM((2, 4, n_y, n_z), F32),
             pltpu.VMEM((n_x, 8, n_z), F32),
             pltpu.VMEM((n_x, 8, n_z), F32),
+            pltpu.VMEM((n_x, n_y + 16, n_z), F32),
             pltpu.SemaphoreType.DMA((n_f + 2,)),
         ],
         compiler_params=pltpu.CompilerParams(vmem_limit_bytes=24 << 20),

time: 25.2 us -> 25 us (level)
  Pallas kernels: 24.5 us -> 24.2 us
where the time goes in v6:
time: 25 us; the launch traced here: 24.9 us
  Pallas kernels  24.2 us (97%)
  between operations  0.64 us (3%)
    pallas_call x1, Pallas kernels, per_device(): pl.pallas_call(functools.partial(droplet_kernel, n_gx, n_gy), out_shape=(...  22.4 us
    pallas_call x1, Pallas kernels, per_device(): pl.pallas_call(edge_kernel, out_shape=(shape((n_f,) + cube), shape((5, SL...  1.79 us

profile of v6, /device:TPU:96, one launch (start us, length us, event | category | flops | bytes accessed | tf_op | source)
XLA Modules:
  0.0 24.9 jit_solution(4352883284442292616)
XLA Ops:
  0.6 22.4 %droplets.1 = (f32[14,16,16,128]{3,2,1,0:T(8,128)S(1)}, f32[2,14,4,16,128]{4,3,2,1,0:T(8,128)S(1)}, f32[14,16,2,4,128]{4,3,2,1,0:T(4,128)S(1)}, f32[5,9216]{1,0:T(8,128)S(1)}, s32[72,128]{1,0:T(8,128)S(1)}) custom-call(f32[14,16,16,128]{3,2,1,0:T(8,128)} %fields.1, f32[14,16,4,4,128]{4,3,2,1,0:T(4,128)} %bitcast.6, f32[5,8192]{1,0:T(8,128)} %state.1, ...), custom_call_target="tpu_custom_call" | custom-call | tf_op jit(solution)/shard_map/droplets/pallas_call | solution.py:443
  23.1 1.8 %edges.1 = (f32[14,16,16,128]{3,2,1,0:T(8,128)}, f32[5,9216]{1,0:T(8,128)}, s32[72,128]{1,0:T(8,128)}) custom-call(f32[14,16,16,128]{3,2,1,0:T(8,128)S(1)} %get-tuple-element.11.part, f32[2,14,4,16,128]{4,3,2,1,0:T(8,128)S(1)} %get-tuple-element.12.xh, f32[14,16,8,128]{3,2,1,0:T(8,128)S(1)} %bitcast.5, f32[5,9216]{1,0:T(8,128)S(1)} %get-tuple-element.14.drops, ...), custom_call_target="tpu_custom_call" | custom-call | tf_op jit(solution)/shard_map/edges/pallas_call | solution.py:498

commit v7 on v6

--- a/solution.py
+++ b/solution.py
@@ -394,11 +394,20 @@
     for x in range(16):
         fy[x, 8:24] = jnp.zeros((16, 128), F32)
     for f in range(N_F):
-
-        def y_step(x, carry):
+        low_x = [flux(f, 0, xh[0, f, i], ux[0, i], px[0, i]) for i in range(4)]
+        high_x = [flux(f, 0, xh[1, f, i], ux[1, i], px[1, i]) for i in range(4)]
+        for x in range(16):
             edge = flux(f, 1, yh[f, x], uy[x], py[x])
             fy[x, 0:8] = edge
             fy[x, 24:32] = edge
+        for x in range(16):
+            base = part[f, x]
+            if x < 4:
+                for k in range(x, 4):
+                    base = base + STENCIL[k] * low_x[3 + x - k]
+            if x >= 12:
+                for k in range(15 - x, 4):
+                    base = base - STENCIL[k] * high_x[k - (15 - x)]
             low = None
             high = None
             for k in range(4):
@@ -406,24 +415,8 @@
                 low = term if low is None else low + term
                 term = STENCIL[k] * fy[x, 17 + k : 25 + k]
                 high = term if high is None else high + term
-            out[f, x, 0:8] = part[f, x, 0:8] + low
-            out[f, x, 8:16] = part[f, x, 8:16] - high
-            return carry
-
-        lax.fori_loop(0, 16, y_step, 0, unroll=16)
-        low = [flux(f, 0, xh[0, f, i], ux[0, i], px[0, i]) for i in range(4)]
-        high = [flux(f, 0, xh[1, f, i], ux[1, i], px[1, i]) for i in range(4)]
-        for x in range(4):
-            total = None
-            for k in range(x, 4):
-                term = STENCIL[k] * low[3 + x - k]
-                total = term if total is None else total + term
-            out[f, x] += total
-            total = None
-            for k in range(x, 4):
-                term = STENCIL[k] * high[k - x]
-                total = term if total is None else total + term
-            out[f, 15 - x] -= total
+            out[f, x, 0:8] = base[0:8] + low
+            out[f, x, 8:16] = base[8:16] - high
         copy = pltpu.make_async_copy(out.at[f], out_h.at[f], sem.at[f])
         copy.start()
         copies.append(copy)

time: 25 us -> 24.9 us (level)
  no operation moved by 1% of the time
where the time goes in v7:
time: 24.9 us; the launch traced here: 24.8 us
  Pallas kernels  24.1 us (97%)
  between operations  0.64 us (3%)
    pallas_call x1, Pallas kernels, per_device(): pl.pallas_call(functools.partial(droplet_kernel, n_gx, n_gy), out_shape=(...  22.4 us
    pallas_call x1, Pallas kernels, per_device(): pl.pallas_call(edge_kernel, out_shape=(shape((n_f,) + cube), shape((5, SL...  1.71 us

profile of v7, /device:TPU:96, one launch (start us, length us, event | category | flops | bytes accessed | tf_op | source)
XLA Modules:
  0.0 24.8 jit_solution(1248270296749702083)
XLA Ops:
  0.6 22.4 %droplets.1 = (f32[14,16,16,128]{3,2,1,0:T(8,128)S(1)}, f32[2,14,4,16,128]{4,3,2,1,0:T(8,128)S(1)}, f32[14,16,2,4,128]{4,3,2,1,0:T(4,128)S(1)}, f32[5,9216]{1,0:T(8,128)S(1)}, s32[72,128]{1,0:T(8,128)S(1)}) custom-call(f32[14,16,16,128]{3,2,1,0:T(8,128)} %fields.1, f32[14,16,4,4,128]{4,3,2,1,0:T(4,128)} %bitcast.6, f32[5,8192]{1,0:T(8,128)} %state.1, ...), custom_call_target="tpu_custom_call" | custom-call | tf_op jit(solution)/shard_map/droplets/pallas_call | solution.py:436
  23.1 1.7 %edges.1 = (f32[14,16,16,128]{3,2,1,0:T(8,128)}, f32[5,9216]{1,0:T(8,128)}, s32[72,128]{1,0:T(8,128)}) custom-call(f32[14,16,16,128]{3,2,1,0:T(8,128)S(1)} %get-tuple-element.11.part, f32[2,14,4,16,128]{4,3,2,1,0:T(8,128)S(1)} %get-tuple-element.12.xh, f32[14,16,8,128]{3,2,1,0:T(8,128)S(1)} %bitcast.5, f32[5,9216]{1,0:T(8,128)S(1)} %get-tuple-element.14.drops, ...), custom_call_target="tpu_custom_call" | custom-call | tf_op jit(solution)/shard_map/edges/pallas_call | solution.py:491
